TPU v7x, 256 devices: a whole 4x4x8 slice. The times are simulated.
256 devices in a mesh: energy: 2 (over core), space: 128 (over z, y, x).
Axes of the slice: x: 4, y: 4, z: 8, core: 2. Of those that a mesh axis runs over, the one named last changes fastest.
Arguments:
- precond: bfloat16 [2, 256, 2, 512, 512], P('energy', 'space'), may hold values from -2 to 2
- coupling: bfloat16 [256, 2, 512, 512], P('space'), may hold values from -0.046875 to 0.046875
- source: float32 [2, 256, 2, 512, 128], P('energy', 'space'), may hold values from -6 to 6
- sigma_ret: float32 [2, 256, 2, 512], P('energy', 'space'), may hold values from -0.4 to 0.4
- occupation: float32 [2, 128], replicated, may hold values from 0.05 to 0.95
- shift_offsets: int32 [2, 4], replicated, may hold values from -1 to 1, as said below
- shift_weights: float32 [2, 4], replicated, may hold values from 0.3 to 3
Outputs:
- sigma_lesser: bfloat16 [2, 256, 2, 512, 512], P('energy', 'space')
- sigma_greater: bfloat16 [2, 256, 2, 512, 512], P('energy', 'space')
Inputs may be any that keep to these rules, and one draw needn't show every extreme that they name: `shift_offsets`: in every energy's list one offset is -1 or 1.
All inputs are finite; a program needn't handle non-finite values.
Results may differ from a plain program's by a relative error of at most 0.015.
Values may be sent and summed in bfloat16 or wider, within the bound.
A program may use at most 64 MiB of HBM per device.

v0:
```python
import jax
import jax.numpy as jnp
from jax import lax
from jax.sharding import PartitionSpec as P

SWEEPS = 4


def from_behind(block, axis, distance):
    devices = range(lax.axis_size(axis))
    route = [(i - distance, i) for i in devices if i - distance in devices]
    return lax.ppermute(block, axis, route)


def extended(array, sides, width):
    for axis, dim in sides:
        peers, length = (lax.axis_size(axis), array.shape[dim])
        up = [(i, (i + 1) % peers) for i in range(peers - 1)]
        down = [(j, i) for i, j in up]
        last = lax.slice_in_dim(array, length - width, length, axis=dim)
        first = lax.slice_in_dim(array, 0, width, axis=dim)
        before = lax.ppermute(last, axis, up)
        after = lax.ppermute(first, axis, down)
        array = jnp.concatenate([before, array, after], axis=dim)
    return array


def multiply(first_operand, second_operand):
    return jnp.einsum(
        "...mn,...nk->...mk", first_operand, second_operand, preferred_element_type=jnp.float32
    )


def multiply_adjoint(first_operand, second_operand):
    return jnp.einsum(
        "...nm,...nk->...mk", first_operand, second_operand, preferred_element_type=jnp.float32
    )


def complex_product(matrix, states):
    real_part = multiply(matrix[..., 0, :, :], states[..., 0, :, :]) - multiply(
        matrix[..., 1, :, :], states[..., 1, :, :]
    )
    imag_part = multiply(matrix[..., 0, :, :], states[..., 1, :, :]) + multiply(
        matrix[..., 1, :, :], states[..., 0, :, :]
    )
    return jnp.stack([real_part, imag_part], axis=-3)


def adjoint_product(matrix, states):
    real_part = multiply_adjoint(matrix[..., 0, :, :], states[..., 0, :, :]) + multiply_adjoint(
        matrix[..., 1, :, :], states[..., 1, :, :]
    )
    imag_part = multiply_adjoint(matrix[..., 0, :, :], states[..., 1, :, :]) - multiply_adjoint(
        matrix[..., 1, :, :], states[..., 0, :, :]
    )
    return jnp.stack([real_part, imag_part], axis=-3)


def self_block(picked, scale):
    scaled = (picked * scale[:, :, None, None, None, :]).astype(jnp.bfloat16)
    real_part = jnp.einsum(
        "ejsmk,ejsnk->esmn",
        picked[:, :, :, 0],
        scaled[:, :, :, 0],
        preferred_element_type=jnp.float32,
    )
    real_part = real_part + jnp.einsum(
        "ejsmk,ejsnk->esmn",
        picked[:, :, :, 1],
        scaled[:, :, :, 1],
        preferred_element_type=jnp.float32,
    )
    imag_part = jnp.einsum(
        "ejsmk,ejsnk->esmn",
        picked[:, :, :, 1],
        scaled[:, :, :, 0],
        preferred_element_type=jnp.float32,
    )
    imag_part = imag_part - jnp.einsum(
        "ejsmk,ejsnk->esmn",
        picked[:, :, :, 0],
        scaled[:, :, :, 1],
        preferred_element_type=jnp.float32,
    )
    return jnp.stack([real_part, imag_part], axis=2).astype(jnp.bfloat16)


def body(precond, coupling, source, sigma_ret, occupation, shift_offsets, shift_weights):
    local_count = source.shape[0]
    mode_count = source.shape[-1]
    energy_total = occupation.shape[0]
    states = complex_product(precond, source.astype(jnp.bfloat16)).astype(jnp.bfloat16)
    sigma_real = sigma_ret[:, :, 0, :, None]
    sigma_imag = sigma_ret[:, :, 1, :, None]
    for sweep_index in range(1, SWEEPS):
        following = from_behind(states[:, 0], "space", -1)
        beyond = jnp.concatenate([states[:, 1:], following[:, None]], axis=1)
        upper_term = complex_product(coupling, beyond)
        handed = adjoint_product(coupling, states).astype(jnp.bfloat16)
        arriving = from_behind(handed[:, -1], "space", 1)
        lower_term = jnp.concatenate([arriving[:, None], handed[:, :-1]], axis=1)
        states_real = states[:, :, 0].astype(jnp.float32)
        states_imag = states[:, :, 1].astype(jnp.float32)
        local_term = jnp.stack(
            [
                sigma_real * states_real - sigma_imag * states_imag,
                sigma_real * states_imag + sigma_imag * states_real,
            ],
            axis=2,
        )
        driven = (source + local_term + upper_term + lower_term.astype(jnp.float32)).astype(
            jnp.bfloat16
        )
        states = complex_product(precond, driven).astype(jnp.bfloat16)
    first_energy = lax.axis_index("energy") * local_count
    local_ids = first_energy + jnp.arange(local_count, dtype=jnp.int32)
    offsets = lax.dynamic_slice_in_dim(shift_offsets, first_energy, local_count, 0)
    weights_here = lax.dynamic_slice_in_dim(shift_weights, first_energy, local_count, 0)
    targets = local_ids[:, None] + offsets
    inside = (targets >= 0) & (targets < energy_total)
    clipped = jnp.clip(targets, 0, energy_total - 1)
    gathered = extended(states, (("energy", 0),), local_count)
    picked = jnp.take(gathered, targets - first_energy + local_count, axis=0)
    occupied = jnp.take(occupation, clipped, axis=0)
    weights = jnp.where(inside, weights_here, jnp.zeros_like(weights_here)) / mode_count
    sigma_lesser = self_block(picked, weights[:, :, None] * occupied)
    sigma_greater = self_block(picked, weights[:, :, None] * (1.0 - occupied))
    return (sigma_lesser, sigma_greater)


def solution(mesh):
    placed = (
        P("energy", "space", None, None, None),
        P("space", None, None, None),
        P("energy", "space", None, None, None),
        P("energy", "space", None, None),
        P(),
        P(),
        P(),
    )
    return jax.shard_map(
        body,
        mesh=mesh,
        in_specs=placed,
        out_specs=(P("energy", "space", None, None, None), P("energy", "space", None, None, None)),
        check_vma=False,
    )
```

profile of v0, /device:TPU:129, one launch (start us, length us, event | category | flops | bytes accessed | tf_op | source)
XLA Modules:
  0.0 97.7 jit_solution(6968177247598977560)
XLA Ops:
  0.7 1.4 %copy.308 = bf16[1,2,2,512,128]{4,3,1,2,0:T(8,128)(2,1)S(1)} copy(f32[1,2,2,512,128]{4,3,2,1,0:T(8,128)} %param.9) | data formatting | bytes 1572864 | tf_op args[2]
  2.1 1.7 %fusion.103 = f32[2,512,128]{2,1,0:T(8,128)S(1)} fusion(bf16[1,2,2,512,128]{4,3,1,2,0:T(8,128)(2,1)S(1)} %copy.308, bf16[1,2,2,512,512]{4,3,2,1,0:T(8,128)(2,1)} %param.7), kind=kOutput, calls=%fused_computation.144 | convolution fusion | flops 134217728 | bytes 1835008 | tf_op jit(solution)/shard_map/...mn,...nk->...mk/dot_general | solution.py:29
  4.7 1.2 %fusion.111 = (f32[1,2,1,512,128]{4,3,1,2,0:T(8,128)S(1)}, f32[1,2,1,512,128]{4,3,1,2,0:T(8,128)}, bf16[2,512,128]{2,1,0:T(8,128)(2,1)S(1)}) fusion(f32[2,512]{1,0:T(2,128)S(1)} %get-tuple-element.33, f32[2,512]{1,0:T(2,128)S(1)} %get-tuple-element.34, bf16[2,512,128]{2,1,0:T(8,128)(2,1)S(1)} %fusion.16, f32[2,512,128]{2,1,0:T(8,128)S(1)} %fusion.103, ...), kind=kOutput, calls=%fused_computation.165 | convolution fusion | flops 135528448 | bytes 3416064 | tf_op jit(solution)/shard_map/...mn,...nk->...mk/dot_general | solution.py:29
  6.0 0.7 fusion.143
  6.7 6.4 %collective-permute-start = (bf16[1,2,512,128]{3,2,1,0:T(8,128)(2,1)}, bf16[1,2,512,128]{3,2,1,0:T(8,128)(2,1)}, u32[]{:S(2)}, u32[]{:S(2)}) collective-permute-start(bf16[1,2,512,128]{3,2,1,0:T(8,128)(2,1)} %get-tuple-element.22), channel_id=1, source_target_pairs={{1,0},{2,1},{3,2},{4,3},{5,4},{6,5},{7,6},{8,7},{9,8},{10,9},{11,1... | collective-permute-start | bytes 786440 | tf_op jit(solution)/shard_map/ppermute | solution.py:12
  13.1 0.5 fusion.76
  13.6 0.5 fusion.78
  14.2 0.5 fusion.36
  14.7 0.5 fusion.37
  15.3 0.7 fusion.133
  16.0 1.9 %collective-permute-start.1 = (bf16[1,2,512,128]{3,2,1,0:T(8,128)(2,1)}, bf16[1,2,512,128]{3,2,1,0:T(8,128)(2,1)}, u32[]{:S(2)}, u32[]{:S(2)}) collective-permute-start(bf16[1,2,512,128]{3,2,1,0:T(8,128)(2,1)} %fusion.133), channel_id=1, source_target_pairs={{0,1},{1,2},{2,3},{3,4},{4,5},{5,6},{6,7},{7,8},{8,9},{9,10},{10,1... | collective-permute-start | bytes 786440 | tf_op jit(solution)/shard_map/ppermute | solution.py:12
  18.4 1.3 %fusion.66 = f32[2,128,512]{1,2,0:T(8,128)S(1)} fusion(bf16[1,1,2,512,128]{4,3,2,1,0:T(8,128)(2,1)S(1)} %get-tuple-element.23, bf16[1,1,2,512,128]{4,3,2,1,0:T(8,128)(2,1)} %bitcast.8, bf16[2,2,512,512]{3,2,1,0:T(8,128)(2,1)S(1)} %copy-done.1), kind=kOutput, calls=%fused_computation.107 | convolution fusion | flops 134742016 | bytes 2097152 | tf_op jit(solution)/shard_map/...mn,...nk->...mk/dot_general | solution.py:29
  19.7 1.3 %fusion.50 = f32[2,128,512]{1,2,0:T(8,128)S(1)} fusion(bf16[1,1,2,512,128]{4,3,2,1,0:T(8,128)(2,1)S(1)} %get-tuple-element.23, bf16[1,1,2,512,128]{4,3,2,1,0:T(8,128)(2,1)} %bitcast.8, bf16[2,2,512,512]{3,2,1,0:T(8,128)(2,1)S(1)} %copy-done.1), kind=kOutput, calls=%fused_computation.91 | convolution fusion | flops 134742016 | bytes 2097152 | tf_op jit(solution)/shard_map/...mn,...nk->...mk/dot_general | solution.py:29
  21.1 1.5 %fusion.15 = f32[1,2,1,512,128]{4,3,1,2,0:T(8,128)S(1)} fusion(f32[2,128,512]{1,2,0:T(8,128)S(1)} %fusion.66, bf16[1,1,2,512,128]{4,3,2,1,0:T(8,128)(2,1)} %bitcast.8, bf16[1,1,2,512,128]{4,3,2,1,0:T(8,128)(2,1)S(1)} %get-tuple-element.23, bf16[2,2,512,512]{3,2,1,0:T(8,128)(2,1)S(1)} %copy-done.1), kind=kOutput, calls=%fused_computation.37 | convolution fusion | flops 134873088 | bytes 2621440 | tf_op jit(solution)/shard_map/...mn,...nk->...mk/dot_general | solution.py:29
  22.6 1.3 %fusion.14 = f32[1,2,1,512,128]{4,3,1,2,0:T(8,128)S(1)} fusion(f32[2,128,512]{1,2,0:T(8,128)S(1)} %fusion.50, bf16[1,1,2,512,128]{4,3,2,1,0:T(8,128)(2,1)} %bitcast.8, bf16[1,1,2,512,128]{4,3,2,1,0:T(8,128)(2,1)S(1)} %get-tuple-element.23, bf16[2,2,512,512]{3,2,1,0:T(8,128)(2,1)S(1)} %copy-done.1), kind=kOutput, calls=%fused_computation.35 | convolution fusion | flops 134873088 | bytes 2621440 | tf_op jit(solution)/shard_map/...mn,...nk->...mk/dot_general | solution.py:29
  23.9 6.6 %collective-permute-done.1 = bf16[1,2,512,128]{3,2,1,0:T(8,128)(2,1)} collective-permute-done((bf16[1,2,512,128]{3,2,1,0:T(8,128)(2,1)}, bf16[1,2,512,128]{3,2,1,0:T(8,128)(2,1)}, u32[]{:S(2)}, u32[]{:S(2)}) %collective-permute-start.1) | collective-permute-done | bytes 262176 | tf_op jit(solution)/shard_map/ppermute | solution.py:12
  30.5 1.4 %fusion.40 = bf16[1,2,2,512,128]{4,3,1,2,0:T(8,128)(2,1)S(1)} fusion(f32[1,2,1,512,128]{4,3,1,2,0:T(8,128)S(1)} %copy-done.5, f32[1,2,1,512,128]{4,3,1,2,0:T(8,128)S(1)} %get-tuple-element.16, f32[1,2,1,512,128]{4,3,1,2,0:T(8,128)S(1)} %fusion.14, f32[1,2,1,512,128]{4,3,1,2,0:T(8,128)S(1)} %fusion.15, f32[1,2,2,512,128]{4,3,2,1,0:T(8,128)S(1)} %copy-done.4, ...), kind=kLoop, calls=%fused_computation.79 | loop fusion | flops 2359296 | bytes 4456448 | tf_op jit(solution)/shard_map/convert_element_type | solution.py:112
  34.0 0.7 fusion.113
  35.2 0.5 fusion.35
  35.8 3.0 %collective-permute-start.2 = (bf16[1,2,512,128]{3,2,1,0:T(8,128)(2,1)S(1)}, bf16[1,2,512,128]{3,2,1,0:T(8,128)(2,1)S(1)}, u32[]{:S(2)}, u32[]{:S(2)}) collective-permute-start(bf16[1,2,512,128]{3,2,1,0:T(8,128)(2,1)S(1)} %get-tuple-element.20), channel_id=1, source_target_pairs={{1,0},{2,1},{3,2},{4,3},{5,4},{6,5},{7,6},{8,7},{9,8},{10,9},{11,1... | collective-permute-start | bytes 786440 | tf_op jit(solution)/shard_map/ppermute | solution.py:12
  38.8 0.5 fusion.34
  39.4 2.5 %collective-permute-start.3 = (bf16[1,2,512,128]{3,2,1,0:T(8,128)(2,1)S(1)}, bf16[1,2,512,128]{3,2,1,0:T(8,128)(2,1)S(1)}, u32[]{:S(2)}, u32[]{:S(2)}) collective-permute-start(bf16[1,2,512,128]{3,2,1,0:T(8,128)(2,1)S(1)} %fusion.127), channel_id=1, source_target_pairs={{0,1},{1,2},{2,3},{3,4},{4,5},{5,6},{6,7},{7,8},{8,9},{9,10},{10,1... | collective-permute-start | bytes 786440 | tf_op jit(solution)/shard_map/ppermute | solution.py:12
  41.9 1.8 %collective-permute-done.2 = bf16[1,2,512,128]{3,2,1,0:T(8,128)(2,1)S(1)} collective-permute-done((bf16[1,2,512,128]{3,2,1,0:T(8,128)(2,1)S(1)}, bf16[1,2,512,128]{3,2,1,0:T(8,128)(2,1)S(1)}, u32[]{:S(2)}, u32[]{:S(2)}) %collective-permute-start.2) | collective-permute-done | bytes 262176 | tf_op jit(solution)/shard_map/ppermute | solution.py:12
  45.4 7.3 %collective-permute-done.3 = bf16[1,2,512,128]{3,2,1,0:T(8,128)(2,1)S(1)} collective-permute-done((bf16[1,2,512,128]{3,2,1,0:T(8,128)(2,1)S(1)}, bf16[1,2,512,128]{3,2,1,0:T(8,128)(2,1)S(1)}, u32[]{:S(2)}, u32[]{:S(2)}) %collective-permute-start.3) | collective-permute-done | bytes 262176 | tf_op jit(solution)/shard_map/ppermute | solution.py:12
  54.7 0.7 fusion.115
  55.4 0.5 fusion.62
  55.9 0.5 fusion.33
  56.5 1.9 %collective-permute-start.4 = (bf16[1,2,512,128]{3,2,1,0:T(8,128)(2,1)S(1)}, bf16[1,2,512,128]{3,2,1,0:T(8,128)(2,1)S(1)}, u32[]{:S(2)}, u32[]{:S(2)}) collective-permute-start(bf16[1,2,512,128]{3,2,1,0:T(8,128)(2,1)S(1)} %get-tuple-element.18), channel_id=1, source_target_pairs={{1,0},{2,1},{3,2},{4,3},{5,4},{6,5},{7,6},{8,7},{9,8},{10,9},{11,1... | collective-permute-start | bytes 786440 | tf_op jit(solution)/shard_map/ppermute | solution.py:12
  58.5 0.5 fusion.32
  59.0 3.4 %collective-permute-start.5 = (bf16[1,2,512,128]{3,2,1,0:T(8,128)(2,1)S(1)}, bf16[1,2,512,128]{3,2,1,0:T(8,128)(2,1)S(1)}, u32[]{:S(2)}, u32[]{:S(2)}) collective-permute-start(bf16[1,2,512,128]{3,2,1,0:T(8,128)(2,1)S(1)} %fusion.121), channel_id=1, source_target_pairs={{0,1},{1,2},{2,3},{3,4},{4,5},{5,6},{6,7},{7,8},{8,9},{9,10},{10,1... | collective-permute-start | bytes 786440 | tf_op jit(solution)/shard_map/ppermute | solution.py:12
  62.4 1.2 %collective-permute-done.4 = bf16[1,2,512,128]{3,2,1,0:T(8,128)(2,1)S(1)} collective-permute-done((bf16[1,2,512,128]{3,2,1,0:T(8,128)(2,1)S(1)}, bf16[1,2,512,128]{3,2,1,0:T(8,128)(2,1)S(1)}, u32[]{:S(2)}, u32[]{:S(2)}) %collective-permute-start.4) | collective-permute-done | bytes 262176 | tf_op jit(solution)/shard_map/ppermute | solution.py:12
  65.4 6.2 %collective-permute-done.5 = bf16[1,2,512,128]{3,2,1,0:T(8,128)(2,1)S(1)} collective-permute-done((bf16[1,2,512,128]{3,2,1,0:T(8,128)(2,1)S(1)}, bf16[1,2,512,128]{3,2,1,0:T(8,128)(2,1)S(1)}, u32[]{:S(2)}, u32[]{:S(2)}) %collective-permute-start.5) | collective-permute-done | bytes 262176 | tf_op jit(solution)/shard_map/ppermute | solution.py:12
  73.8 5.8 %collective-permute-start.7 = (bf16[1,2,2,512,128]{3,4,1,2,0:T(8,128)(2,1)S(1)}, bf16[1,2,2,512,128]{3,4,1,2,0:T(8,128)(2,1)S(1)}, u32[]{:S(2)}, u32[]{:S(2)}) collective-permute-start(bf16[1,2,2,512,128]{3,4,1,2,0:T(8,128)(2,1)S(1)} %pad_maximum_fusion.6), channel_id=1, source_target_pairs={{128,0},{129,1},{130,2},{131,3},{132,4},{133,5},{134,6},{135,7},{1... | collective-permute-start | bytes 1572872 | tf_op jit(solution)/shard_map/ppermute | solution.py:23
  79.6 1.5 %collective-permute-start.6 = (bf16[1,2,2,512,128]{3,4,1,2,0:T(8,128)(2,1)S(1)}, bf16[1,2,2,512,128]{3,4,1,2,0:T(8,128)(2,1)S(1)}, u32[]{:S(2)}, u32[]{:S(2)}) collective-permute-start(bf16[1,2,2,512,128]{3,4,1,2,0:T(8,128)(2,1)S(1)} %pad_maximum_fusion.6), channel_id=1, source_target_pairs={{0,128},{1,129},{2,130},{3,131},{4,132},{5,133},{6,134},{7,135},{8... | collective-permute-start | bytes 1572872 | tf_op jit(solution)/shard_map/ppermute | solution.py:22
  81.2 0.6 gather_fusion.1
  81.9 1.6 %collective-permute-done.6 = bf16[1,2,2,512,128]{3,4,1,2,0:T(8,128)(2,1)S(1)} collective-permute-done((bf16[1,2,2,512,128]{3,4,1,2,0:T(8,128)(2,1)S(1)}, bf16[1,2,2,512,128]{3,4,1,2,0:T(8,128)(2,1)S(1)}, u32[]{:S(2)}, u32[]{:S(2)}) %collective-permute-start.6) | collective-permute-done | bytes 524320 | tf_op jit(solution)/shard_map/ppermute | solution.py:22
  83.6 2.0 %gather_fusion = bf16[4,2,2,512,128]{3,4,1,2,0:T(8,128)(2,1)} fusion(bf16[3,2,2,512,128]{3,4,1,2,0:T(8,128)(2,1)S(1)} %pad_maximum_fusion.2, s32[1024]{0:T(1024)S(1)} %pad_clamp_fusion.1), kind=kCustom, calls=%fused_computation | custom fusion | bytes 4194320 | tf_op jit(solution)/shard_map/jit(_take)/gather | solution.py:124
  85.6 2.2 %fusion.1 = (bf16[1,4,2,2,512,128]{4,5,2,3,1,0:T(8,128)(2,1)S(1)}, bf16[1,4,2,2,512,128]{4,5,2,3,1,0:T(8,128)(2,1)S(1)}) fusion(f32[4,128]{1,0:T(4,128)S(1)} %get-tuple-element.27, bf16[4,2,2,512,128]{3,4,1,2,0:T(8,128)(2,1)} %gather_fusion, pred[4]{0:T(512)(128)(4,1)S(1)} %get-tuple-element.10), kind=kLoop, calls=%fused_computation.5 | loop fusion | flops 4194304 | bytes 6293508 | tf_op jit(solution)/shard_map/convert_element_type | solution.py:61
  88.2 0.8 fusion.107
  89.0 0.8 fusion.108
  89.8 0.8 fusion.109
  90.5 0.8 fusion.110
  91.3 0.8 fusion.7
  92.1 0.8 fusion.6
  93.1 1.5 %copy.207 = bf16[1,2,2,512,512]{4,3,2,1,0:T(8,128)(2,1)} copy(bf16[1,2,2,512,512]{4,3,1,2,0:T(8,128)(2,1)S(1)} %pad_maximum_fusion) | data formatting | bytes 4194304
  94.5 0.8 fusion.9
  95.3 0.8 fusion.8
  96.2 1.5 %copy.208 = bf16[1,2,2,512,512]{4,3,2,1,0:T(8,128)(2,1)} copy(bf16[1,2,2,512,512]{4,3,1,2,0:T(8,128)(2,1)S(1)} %pad_maximum_fusion.1) | data formatting | bytes 4194304
  (61 shorter events, 12.9 us)
Async XLA Ops:
  0.6 80.5 %copy-start = (f32[2,128]{1,0:T(2,128)S(1)}, f32[2,128]{1,0:T(2,128)}, u32[]{:S(2)}) copy-start(f32[2,128]{1,0:T(2,128)} %param.11) | copy-start | bytes 3076
  0.6 3.1 %copy-start.2 = (bf16[1,2,2,512,512]{4,3,2,1,0:T(8,128)(2,1)S(1)}, bf16[1,2,2,512,512]{4,3,2,1,0:T(8,128)(2,1)}, u32[]{:S(2)}) copy-start(bf16[1,2,2,512,512]{4,3,2,1,0:T(8,128)(2,1)} %param.7) | copy-start | bytes 6291460
  2.1 2.1 %copy-start.6 = (f32[1,2,2,512]{3,2,1,0:T(2,128)S(1)}, f32[1,2,2,512]{3,2,1,0:T(2,128)}, u32[]{:S(2)}) copy-start(f32[1,2,2,512]{3,2,1,0:T(2,128)} %param.10) | copy-start | bytes 24580
  4.7 8.4 %copy-start.1 = (bf16[2,2,512,512]{3,2,1,0:T(8,128)(2,1)S(1)}, bf16[2,2,512,512]{3,2,1,0:T(8,128)(2,1)}, u32[]{:S(2)}) copy-start(bf16[2,2,512,512]{3,2,1,0:T(8,128)(2,1)} %param.8) | copy-start | bytes 6291460
  6.7 11.6 %collective-permute-start = (bf16[1,2,512,128]{3,2,1,0:T(8,128)(2,1)}, bf16[1,2,512,128]{3,2,1,0:T(8,128)(2,1)}, u32[]{:S(2)}, u32[]{:S(2)}) collective-permute-start(bf16[1,2,512,128]{3,2,1,0:T(8,128)(2,1)} %get-tuple-element.22), channel_id=1, source_target_pairs={{1,0},{2,1},{3,2},{4,3},{5,4},{6,5},{7,6},{8,7},{9,8},{10,9},{11,1... | collective-permute-start | bytes 786440 | tf_op jit(solution)/shard_map/ppermute | solution.py:12
  14.2 3.7 %copy-start.7 = (s32[2,4]{1,0:T(2,128)S(1)}, s32[2,4]{1,0:T(2,128)}, u32[]{:S(2)}) copy-start(s32[2,4]{1,0:T(2,128)} %param.12) | copy-start | bytes 100
  16.0 14.5 %collective-permute-start.1 = (bf16[1,2,512,128]{3,2,1,0:T(8,128)(2,1)}, bf16[1,2,512,128]{3,2,1,0:T(8,128)(2,1)}, u32[]{:S(2)}, u32[]{:S(2)}) collective-permute-start(bf16[1,2,512,128]{3,2,1,0:T(8,128)(2,1)} %fusion.133), channel_id=1, source_target_pairs={{0,1},{1,2},{2,3},{3,4},{4,5},{5,6},{6,7},{7,8},{8,9},{9,10},{10,1... | collective-permute-start | bytes 786440 | tf_op jit(solution)/shard_map/ppermute | solution.py:12
  21.1 9.4 %copy-start.4 = (f32[1,2,2,512,128]{4,3,2,1,0:T(8,128)S(1)}, f32[1,2,2,512,128]{4,3,2,1,0:T(8,128)}, u32[]{:S(2)}) copy-start(f32[1,2,2,512,128]{4,3,2,1,0:T(8,128)} %param.9) | copy-start | bytes 3145732
  21.1 9.4 %copy-start.5 = (f32[1,2,1,512,128]{4,3,1,2,0:T(8,128)S(1)}, f32[1,2,1,512,128]{4,3,1,2,0:T(8,128)}, u32[]{:S(2)}) copy-start(f32[1,2,1,512,128]{4,3,1,2,0:T(8,128)} %get-tuple-element.17) | copy-start | bytes 1572868
  30.5 1.7 %copy-start.3 = (bf16[1,2,2,512,512]{4,3,2,1,0:T(8,128)(2,1)S(1)}, bf16[1,2,2,512,512]{4,3,2,1,0:T(8,128)(2,1)}, u32[]{:S(2)}) copy-start(bf16[1,2,2,512,512]{4,3,2,1,0:T(8,128)(2,1)} %param.7) | copy-start | bytes 6291460
  35.8 7.8 %collective-permute-start.2 = (bf16[1,2,512,128]{3,2,1,0:T(8,128)(2,1)S(1)}, bf16[1,2,512,128]{3,2,1,0:T(8,128)(2,1)S(1)}, u32[]{:S(2)}, u32[]{:S(2)}) collective-permute-start(bf16[1,2,512,128]{3,2,1,0:T(8,128)(2,1)S(1)} %get-tuple-element.20), channel_id=1, source_target_pairs={{1,0},{2,1},{3,2},{4,3},{5,4},{6,5},{7,6},{8,7},{9,8},{10,9},{11,1... | collective-permute-start | bytes 786440 | tf_op jit(solution)/shard_map/ppermute | solution.py:12
  39.4 13.3 %collective-permute-start.3 = (bf16[1,2,512,128]{3,2,1,0:T(8,128)(2,1)S(1)}, bf16[1,2,512,128]{3,2,1,0:T(8,128)(2,1)S(1)}, u32[]{:S(2)}, u32[]{:S(2)}) collective-permute-start(bf16[1,2,512,128]{3,2,1,0:T(8,128)(2,1)S(1)} %fusion.127), channel_id=1, source_target_pairs={{0,1},{1,2},{2,3},{3,4},{4,5},{5,6},{6,7},{7,8},{8,9},{9,10},{10,1... | collective-permute-start | bytes 786440 | tf_op jit(solution)/shard_map/ppermute | solution.py:12
  56.5 7.1 %collective-permute-start.4 = (bf16[1,2,512,128]{3,2,1,0:T(8,128)(2,1)S(1)}, bf16[1,2,512,128]{3,2,1,0:T(8,128)(2,1)S(1)}, u32[]{:S(2)}, u32[]{:S(2)}) collective-permute-start(bf16[1,2,512,128]{3,2,1,0:T(8,128)(2,1)S(1)} %get-tuple-element.18), channel_id=1, source_target_pairs={{1,0},{2,1},{3,2},{4,3},{5,4},{6,5},{7,6},{8,7},{9,8},{10,9},{11,1... | collective-permute-start | bytes 786440 | tf_op jit(solution)/shard_map/ppermute | solution.py:12
  59.0 12.5 %collective-permute-start.5 = (bf16[1,2,512,128]{3,2,1,0:T(8,128)(2,1)S(1)}, bf16[1,2,512,128]{3,2,1,0:T(8,128)(2,1)S(1)}, u32[]{:S(2)}, u32[]{:S(2)}) collective-permute-start(bf16[1,2,512,128]{3,2,1,0:T(8,128)(2,1)S(1)} %fusion.121), channel_id=1, source_target_pairs={{0,1},{1,2},{2,3},{3,4},{4,5},{5,6},{6,7},{7,8},{8,9},{9,10},{10,1... | collective-permute-start | bytes 786440 | tf_op jit(solution)/shard_map/ppermute | solution.py:12
  73.2 8.5 %copy-start.8 = (f32[2,4]{1,0:T(2,128)S(1)}, f32[2,4]{1,0:T(2,128)}, u32[]{:S(2)}) copy-start(f32[2,4]{1,0:T(2,128)} %param.13) | copy-start | bytes 100
  73.8 8.1 %collective-permute-start.7 = (bf16[1,2,2,512,128]{3,4,1,2,0:T(8,128)(2,1)S(1)}, bf16[1,2,2,512,128]{3,4,1,2,0:T(8,128)(2,1)S(1)}, u32[]{:S(2)}, u32[]{:S(2)}) collective-permute-start(bf16[1,2,2,512,128]{3,4,1,2,0:T(8,128)(2,1)S(1)} %pad_maximum_fusion.6), channel_id=1, source_target_pairs={{128,0},{129,1},{130,2},{131,3},{132,4},{133,5},{134,6},{135,7},{1... | collective-permute-start | bytes 1572872 | tf_op jit(solution)/shard_map/ppermute | solution.py:23
  79.6 3.8 %collective-permute-start.6 = (bf16[1,2,2,512,128]{3,4,1,2,0:T(8,128)(2,1)S(1)}, bf16[1,2,2,512,128]{3,4,1,2,0:T(8,128)(2,1)S(1)}, u32[]{:S(2)}, u32[]{:S(2)}) collective-permute-start(bf16[1,2,2,512,128]{3,4,1,2,0:T(8,128)(2,1)S(1)} %pad_maximum_fusion.6), channel_id=1, source_target_pairs={{0,128},{1,129},{2,130},{3,131},{4,132},{5,133},{6,134},{7,135},{8... | collective-permute-start | bytes 1572872 | tf_op jit(solution)/shard_map/ppermute | solution.py:22
where the time goes:
time: 98.1 us; the launch traced here: 97.7 us
  matrix products  31.1 us (32%)
  starting transfers between devices  26.4 us (27%)
  waiting for transfers between devices  25 us (25%)
  local copies, waits for them, and re-layouts  7.3 us (7%)
  other arithmetic  6.67 us (7%)
  between operations  1.21 us (1%)
    ppermute x6, waiting for transfers between devices, from_behind(): return lax.ppermute(block, axis, route)  23.4 us
    ppermute x6, starting transfers between devices, from_behind(): return lax.ppermute(block, axis, route)  19 us
    dot_general x28, matrix products, multiply(): jnp.einsum('...mn,...nk->...mk', first_operand, second_operand, preferred...  18.7 us
    dot_general x12, matrix products, multiply_adjoint(): jnp.einsum('...nm,...nk->...mk', first_operand, second_operand, preferred...  6.37 us
    ppermute x1, starting transfers between devices, extended(): after = lax.ppermute(first, axis, down)  5.84 us
    unnamed x22, local copies, waits for them, and re-layouts  4.73 us
    convert_element_type x2, other arithmetic, self_block(): scaled = (picked * scale[:, :, None, None, None, :]).astype(jnp.bfloat16)  2.61 us
    gather x1, local copies, waits for them, and re-layouts, body(): picked = jnp.take(gathered, targets - first_energy + local_count, axis=0)  2 us
  transfers between devices with their start and end apart: 8, of which 7 were waited for; matrix products, arithmetic and copies ran while one was open for 14% of the time, Pallas kernels for 0%

commit v1 on v0

v1 whole, which is shorter than its diff:
```python
import functools

import jax
import jax.numpy as jnp
from jax import lax
from jax.experimental import pallas as pl
from jax.experimental.pallas import tpu as pltpu
from jax.sharding import PartitionSpec as P

SWEEPS = 4
MESH = pl.DeviceIdType.MESH
F32 = jnp.float32
BF16 = jnp.bfloat16


def dot(a, b):
    return jnp.dot(a, b, preferred_element_type=F32)


def dot_t(a, b):
    return lax.dot_general(a, b, (((0,), (0,)), ((), ())), preferred_element_type=F32)


def cprod(mr, mi, sr, si):
    return dot(mr, sr) - dot(mi, si), dot(mr, si) + dot(mi, sr)


def cprod_adj(mr, mi, sr, si):
    return dot_t(mr, sr) + dot_t(mi, si), dot_t(mr, si) - dot_t(mi, sr)


def solve_kernel(n, pre_ref, cpl_ref, src_ref, sig_ref, out_ref,
                 st, follow, arrive, hand, send_sem, recv_sem):
    me = lax.axis_index("space")
    en = lax.axis_index("energy")
    prev = lax.rem(me + n - 1, n)
    nxt = lax.rem(me + 1, n)

    barrier = pltpu.get_barrier_semaphore()
    for peer in (prev, nxt):
        pl.semaphore_signal(barrier, inc=1, device_id=(en, peer), device_id_type=MESH)
    pl.semaphore_wait(barrier, 2)

    @pl.when(me == n - 1)
    def _():
        follow[...] = jnp.zeros_like(follow)

    @pl.when(me == 0)
    def _():
        arrive[...] = jnp.zeros_like(arrive)

    for s in range(2):
        sr = src_ref[0, s, 0].astype(BF16)
        si = src_ref[0, s, 1].astype(BF16)
        re, im = cprod(pre_ref[0, s, 0], pre_ref[0, s, 1], sr, si)
        st[s, 0] = re.astype(BF16)
        st[s, 1] = im.astype(BF16)

    def local(s):
        xr = st[s, 0].astype(F32)
        xi = st[s, 1].astype(F32)
        gr = sig_ref[0, s, 0]
        gi = sig_ref[0, s, 1]
        return (src_ref[0, s, 0] + (gr * xr - gi * xi),
                src_ref[0, s, 1] + (gr * xi + gi * xr))

    for sweep in range(SWEEPS - 1):
        to_prev = pltpu.make_async_remote_copy(
            src_ref=st.at[0], dst_ref=follow.at[sweep],
            send_sem=send_sem.at[0, sweep], recv_sem=recv_sem.at[0, sweep],
            device_id=(en, prev), device_id_type=MESH)
        to_next = pltpu.make_async_remote_copy(
            src_ref=hand.at[sweep], dst_ref=arrive.at[sweep],
            send_sem=send_sem.at[1, sweep], recv_sem=recv_sem.at[1, sweep],
            device_id=(en, nxt), device_id_type=MESH)

        @pl.when(me > 0)
        def _():
            to_prev.start()

        hr, hi = cprod_adj(cpl_ref[1, 0], cpl_ref[1, 1], st[1, 0], st[1, 1])
        hand[sweep, 0] = hr.astype(BF16)
        hand[sweep, 1] = hi.astype(BF16)

        @pl.when(me < n - 1)
        def _():
            to_next.start()

        lr, li = cprod_adj(cpl_ref[0, 0], cpl_ref[0, 1], st[0, 0], st[0, 1])
        lr = lr.astype(BF16).astype(F32)
        li = li.astype(BF16).astype(F32)
        a1r, a1i = local(1)
        ur, ui = cprod(cpl_ref[0, 0], cpl_ref[0, 1], st[1, 0], st[1, 1])
        a0r, a0i = local(0)
        d0r = a0r + ur
        d0i = a0i + ui

        @pl.when(me < n - 1)
        def _():
            to_prev.wait_recv()

        fr, fi = cprod(cpl_ref[1, 0], cpl_ref[1, 1], follow[sweep, 0], follow[sweep, 1])
        d1r = ((a1r + fr) + lr).astype(BF16)
        d1i = ((a1i + fi) + li).astype(BF16)

        @pl.when(me > 0)
        def _():
            to_next.wait_recv()

        d0r = (d0r + arrive[sweep, 0].astype(F32)).astype(BF16)
        d0i = (d0i + arrive[sweep, 1].astype(F32)).astype(BF16)

        @pl.when(me > 0)
        def _():
            to_prev.wait_send()

        @pl.when(me < n - 1)
        def _():
            to_next.wait_send()

        n0r, n0i = cprod(pre_ref[0, 0, 0], pre_ref[0, 0, 1], d0r, d0i)
        n1r, n1i = cprod(pre_ref[0, 1, 0], pre_ref[0, 1, 1], d1r, d1i)
        st[0, 0] = n0r.astype(BF16)
        st[0, 1] = n0i.astype(BF16)
        st[1, 0] = n1r.astype(BF16)
        st[1, 1] = n1i.astype(BF16)

    out_ref[...] = st[...][None]


def solve(precond, coupling, source, sigma, n):
    shape = source.shape[:-1] + (source.shape[-1],)
    sweeps = SWEEPS - 1
    half = (2,) + source.shape[3:]
    vmem = pl.BlockSpec(memory_space=pltpu.VMEM)
    return pl.pallas_call(
        functools.partial(solve_kernel, n),
        out_shape=jax.ShapeDtypeStruct(shape, BF16),
        in_specs=[vmem] * 4,
        out_specs=vmem,
        scratch_shapes=[
            pltpu.VMEM((2,) + half, BF16),
            pltpu.VMEM((sweeps,) + half, BF16),
            pltpu.VMEM((sweeps,) + half, BF16),
            pltpu.VMEM((sweeps,) + half, BF16),
            pltpu.SemaphoreType.DMA((2, sweeps)),
            pltpu.SemaphoreType.DMA((2, sweeps)),
        ],
        compiler_params=pltpu.CompilerParams(collective_id=0, has_side_effects=True),
    )(precond, coupling, source, sigma)


def self_energy(picked, scale):
    scaled = (picked.astype(F32) * scale).astype(BF16)
    pr, pi = picked[:, 0], picked[:, 1]
    br, bi = scaled[:, 0], scaled[:, 1]
    ein = functools.partial(jnp.einsum, "smk,snk->smn", preferred_element_type=F32)
    real_part = ein(pr, br) + ein(pi, bi)
    imag_part = ein(pi, br) - ein(pr, bi)
    return jnp.stack([real_part, imag_part], axis=1).astype(BF16)[None]


def body(precond, coupling, source, sigma_ret, occupation, shift_offsets, shift_weights):
    n = lax.axis_size("space")
    mode_count = source.shape[-1]
    energy_total = occupation.shape[0]
    sigma = sigma_ret[..., None]
    states = solve(precond, coupling, source, sigma, n)
    own = states[0]
    other = lax.ppermute(own, "energy", [(0, 1), (1, 0)])
    e = lax.axis_index("energy")
    offsets = lax.dynamic_index_in_dim(shift_offsets, e, 0, keepdims=False)
    weights_here = lax.dynamic_index_in_dim(shift_weights, e, 0, keepdims=False)
    targets = e + offsets
    inside = (targets >= 0) & (targets < energy_total)
    weights = jnp.where(inside, weights_here, jnp.zeros_like(weights_here)) / mode_count
    coef_own = jnp.sum(jnp.where(targets == e, weights, 0.0))
    coef_other = jnp.sum(jnp.where(targets == 1 - e, weights, 0.0))
    occ_own = lax.dynamic_index_in_dim(occupation, e, 0, keepdims=False)
    occ_other = lax.dynamic_index_in_dim(occupation, 1 - e, 0, keepdims=False)
    picked = jnp.concatenate([own, other], axis=-1)
    less = jnp.concatenate([coef_own * occ_own, coef_other * occ_other])
    great = jnp.concatenate([coef_own * (1.0 - occ_own), coef_other * (1.0 - occ_other)])
    return self_energy(picked, less), self_energy(picked, great)


def solution(mesh):
    placed = (
        P("energy", "space", None, None, None),
        P("space", None, None, None),
        P("energy", "space", None, None, None),
        P("energy", "space", None, None),
        P(),
        P(),
        P(),
    )
    return jax.shard_map(
        body,
        mesh=mesh,
        in_specs=placed,
        out_specs=(P("energy", "space", None, None, None), P("energy", "space", None, None, None)),
        check_vma=False,
    )
```

time: 98.1 us -> 58.3 us (0.59)
  Pallas kernels: 0 us -> 41.6 us
  matrix products: 31.1 us -> 3.78 us
  waiting for transfers between devices: 25 us -> 0.01 us
  starting transfers between devices: 26.4 us -> 3.1 us
  other arithmetic: 6.67 us -> 3.89 us
  local copies, waits for them, and re-layouts: 7.3 us -> 4.96 us
    pallas_call x0 -> x1, Pallas kernels: none -> 41.6 us  [solve(): pl.pallas_call(functools.partial(solve_kernel, n), out_shape=jax.ShapeDty...]
    dot_general x48 -> x8, matrix products: 31.1 us -> 3.78 us  [the longest x4 1.9 us: self_energy(): real_part = ein(pr, br) + ein(pi, bi)]
    ppermute x8 -> x1, waiting for transfers between devices: 25 us -> 0.01 us  [body(): other = lax.ppermute(own, 'energy', [(0, 1), (1, 0)])]
    ppermute x8 -> x1, starting transfers between devices: 26.4 us -> 3.1 us  [body(): other = lax.ppermute(own, 'energy', [(0, 1), (1, 0)])]
    convert_element_type x5 -> x1, other arithmetic: 4.31 us -> 0.42 us  [self_energy(): scaled = (picked.astype(F32) * scale).astype(BF16)]
    gather x2 -> x0, local copies, waits for them, and re-layouts: 2.56 us -> none  [the longest x1 2 us: body(): picked = jnp.take(gathered, targets - first_energy + local_count, axis=0)]
    broadcast_in_dim x0 -> x1, local copies, waits for them, and re-layouts: none -> 2.04 us  [body(): sigma = sigma_ret[..., None]]
    unnamed x22 -> x10, local copies, waits for them, and re-layouts: 4.73 us -> 2.92 us
  transfers between devices with their start and end apart: 8 -> 1, of which waited for: 7 -> 0; matrix products, arithmetic and copies ran while one was open for 14% -> 3% of each run, Pallas kernels for 0% -> 0%
where the time goes in v1:
time: 58.3 us; the launch traced here: 58.1 us
  Pallas kernels  41.6 us (71%)
  local copies, waits for them, and re-layouts  4.96 us (9%)
  other arithmetic  3.89 us (7%)
  matrix products  3.78 us (6%)
  starting transfers between devices  3.1 us (5%)
  between operations  0.75 us (1%)
    pallas_call x1, Pallas kernels, solve(): pl.pallas_call(functools.partial(solve_kernel, n), out_shape=jax.ShapeDty...  41.6 us
    ppermute x1, starting transfers between devices, body(): other = lax.ppermute(own, 'energy', [(0, 1), (1, 0)])  3.1 us
    unnamed x10, local copies, waits for them, and re-layouts  2.92 us
    broadcast_in_dim x1, local copies, waits for them, and re-layouts, body(): sigma = sigma_ret[..., None]  2.04 us
    dot_general x4, matrix products, self_energy(): real_part = ein(pr, br) + ein(pi, bi)  1.9 us
    dot_general x4, matrix products, self_energy(): imag_part = ein(pi, br) - ein(pr, bi)  1.88 us
    mul x1, other arithmetic, body(): coef_own * (1.0 - occ_own)  1.3 us
  transfers between devices with their start and end apart: 1, of which 0 were waited for; matrix products, arithmetic and copies ran while one was open for 3% of the time, Pallas kernels for 0%

profile of v1, /device:TPU:129, one launch (start us, length us, event | category | flops | bytes accessed | tf_op | source)
XLA Modules:
  0.0 58.1 jit_solution(13311563319820153022)
XLA Ops:
  0.6 2.0 %copy.11.sig_ref = f32[1,2,2,512,1]{4,3,2,1,0:T(8,128)} copy(f32[1,2,2,512,1]{3,2,1,4,0:T(2,128)} %bitcast.49) | data formatting | bytes 16384 | tf_op jit(solution)/shard_map/broadcast_in_dim | solution.py:167
  2.7 0.0 copy-start.2
  2.7 0.0 copy-start.3
  2.7 0.0 copy-start.1
  2.7 41.6 %shard_map.86 = bf16[1,2,2,512,128]{4,3,2,1,0:T(8,128)(2,1)} custom-call(bf16[1,2,2,512,512]{4,3,2,1,0:T(8,128)(2,1)} %pre_ref.1, bf16[2,2,512,512]{3,2,1,0:T(8,128)(2,1)} %cpl_ref.1, f32[1,2,2,512,128]{4,3,2,1,0:T(8,128)} %src_ref.1, f32[1,2,2,512,1]{4,3,2,1,0:T(8,128)} %copy.11.sig_ref), custom_call_target="tpu_custom_call" | custom-call | tf_op jit(solution)/shard_map/pallas_call | solution.py:136
  44.3 0.0 copy-start
  44.3 3.1 %collective-permute-start = (bf16[2,2,512,128]{3,2,1,0:T(8,128)(2,1)}, bf16[2,2,512,128]{3,2,1,0:T(8,128)(2,1)S(1)}, u32[]{:S(2)}, u32[]{:S(2)}) collective-permute-start(bf16[2,2,512,128]{3,2,1,0:T(8,128)(2,1)} %bitcast.46), channel_id=1, source_target_pairs={{0,128},{128,0},{1,129},{129,1},{2,130},{130,2},{3,131},{131,3},{4... | collective-permute-start | bytes 1572872 | tf_op jit(solution)/shard_map/ppermute | solution.py:170
  47.4 0.0 copy-done.2
  47.4 0.0 copy-done.3
  47.4 0.6 %fusion.15 = (f32[]{:T(128)}, f32[]{:T(128)}) fusion(s32[]{:T(128)S(6)} %axis_index.15, f32[2,4]{1,0:T(2,128)S(1)} %copy-done.2, s32[]{:T(128)S(6)} %select_n.25, s32[2,4]{1,0:T(2,128)S(1)} %copy-done.3, s32[]{:T(128)S(6)} %sub.18), kind=kLoop, calls=%fused_computation.41 | loop fusion | flops 46 | bytes 52 | tf_op jit(solution)/shard_map/reduce_sum | solution.py:177
  48.0 0.0 copy-done.1
  48.0 1.3 %multiply_bitcast_fusion.1 = (f32[128]{0:T(128)S(1)}, f32[128]{0:T(128)S(1)}, f32[128]{0:T(128)S(1)}, f32[128]{0:T(128)S(1)}) fusion(f32[]{:T(128)} %get-tuple-element.6, f32[2,128]{1,0:T(2,128)S(1)} %copy-done.1, s32[]{:T(128)S(6)} %select_n.25, s32[]{:T(128)S(6)} %select_n.30, f32[]{:T(128)} %get-tuple-element.7), kind=kLoop, calls=%fused_computation.44 | loop fusion | flops 768 | bytes 3088 | tf_op jit(solution)/shard_map/mul | solution.py:183
  49.4 0.0 collective-permute-done
  49.4 1.2 %fusion.9 = (bf16[2,512,256]{2,1,0:T(8,128)(2,1)S(1)}, bf16[2,512,256]{2,1,0:T(8,128)(2,1)S(1)}) fusion(bf16[2,2,512,128]{3,2,1,0:T(8,128)(2,1)} %bitcast.47, bf16[2,2,512,128]{3,2,1,0:T(8,128)(2,1)S(1)} %collective-permute-done), kind=kLoop, calls=%fused_computation.22 | loop fusion | flops 2097152 | bytes 2097152 | tf_op jit(solution)/shard_map/squeeze | solution.py:155
  50.5 0.0 copy-done
  50.5 0.4 fusion.1
  51.0 0.5 fusion.12
  51.4 0.5 fusion.13
  51.9 0.5 fusion.10
  52.4 0.5 fusion.11
  52.8 0.5 fusion.5
  53.3 0.5 fusion.4
  53.8 0.2 pad_maximum_fusion.1
  54.0 1.5 %copy.13 = bf16[1,2,2,512,512]{4,3,2,1,0:T(8,128)(2,1)} copy(bf16[1,2,2,512,512]{4,3,1,2,0:T(8,128)(2,1)S(1)} %pad_maximum_fusion.1) | data formatting | bytes 4194304
  55.5 0.5 fusion.3
  56.0 0.5 fusion.2
  56.4 0.2 pad_maximum_fusion
  56.6 1.5 %copy.12 = bf16[1,2,2,512,512]{4,3,2,1,0:T(8,128)(2,1)} copy(bf16[1,2,2,512,512]{4,3,1,2,0:T(8,128)(2,1)S(1)} %pad_maximum_fusion) | data formatting | bytes 4194304
  (1 shorter events, 0.0 us)
Async XLA Ops:
  2.7 44.7 %copy-start.2 = (f32[2,4]{1,0:T(2,128)S(1)}, f32[2,4]{1,0:T(2,128)}, u32[]{:S(2)}) copy-start(f32[2,4]{1,0:T(2,128)} %param.13) | copy-start | bytes 100
  2.7 44.7 %copy-start.3 = (s32[2,4]{1,0:T(2,128)S(1)}, s32[2,4]{1,0:T(2,128)}, u32[]{:S(2)}) copy-start(s32[2,4]{1,0:T(2,128)} %param.12) | copy-start | bytes 100
  2.7 45.4 %copy-start.1 = (f32[2,128]{1,0:T(2,128)S(1)}, f32[2,128]{1,0:T(2,128)}, u32[]{:S(2)}) copy-start(f32[2,128]{1,0:T(2,128)} %param.11) | copy-start | bytes 3076
  44.3 6.2 %copy-start = (bf16[1,2,2,512,128]{4,3,2,1,0:T(8,128)(2,1)S(1)}, bf16[1,2,2,512,128]{4,3,2,1,0:T(8,128)(2,1)}, u32[]{:S(2)}) copy-start(bf16[1,2,2,512,128]{4,3,2,1,0:T(8,128)(2,1)} %shard_map.86) | copy-start | bytes 1572868
  44.3 5.0 %collective-permute-start = (bf16[2,2,512,128]{3,2,1,0:T(8,128)(2,1)}, bf16[2,2,512,128]{3,2,1,0:T(8,128)(2,1)S(1)}, u32[]{:S(2)}, u32[]{:S(2)}) collective-permute-start(bf16[2,2,512,128]{3,2,1,0:T(8,128)(2,1)} %bitcast.46), channel_id=1, source_target_pairs={{0,128},{128,0},{1,129},{129,1},{2,130},{130,2},{3,131},{131,3},{4... | collective-permute-start | bytes 1572872 | tf_op jit(solution)/shard_map/ppermute | solution.py:170

commit v2 on v1

v2 whole, which is shorter than its diff:
```python
import functools

import jax
import jax.numpy as jnp
from jax import lax
from jax.experimental import pallas as pl
from jax.experimental.pallas import tpu as pltpu
from jax.sharding import PartitionSpec as P

SWEEPS = 4
MESH = pl.DeviceIdType.MESH
F32 = jnp.float32
BF16 = jnp.bfloat16


def dot(a, b):
    return jnp.dot(a, b, preferred_element_type=F32)


def solve_kernel(n, pre_hbm, cpl_hbm, src_hbm, sig_ref, out_ref,
                 pre, cpl, src, ct, st, follow, arrive, hand, other,
                 load_sem, send_sem, recv_sem, swap_sem):
    me = lax.axis_index("space")
    en = lax.axis_index("energy")
    prev = lax.rem(me + n - 1, n)
    nxt = lax.rem(me + 1, n)
    mate = 1 - en
    h = src.shape[-1]

    loads = [pltpu.make_async_copy(src_hbm.at[0], src, load_sem.at[0])]
    loads += [pltpu.make_async_copy(pre_hbm.at[0, s], pre.at[s], load_sem.at[1 + s]) for s in range(2)]
    loads += [pltpu.make_async_copy(cpl_hbm.at[s], cpl.at[s], load_sem.at[3 + s]) for s in range(2)]
    for c in loads:
        c.start()

    barrier = pltpu.get_barrier_semaphore()
    for peer in ((en, prev), (en, nxt), (mate, me)):
        pl.semaphore_signal(barrier, inc=1, device_id=peer, device_id_type=MESH)
    pl.semaphore_wait(barrier, 3)

    @pl.when(me == n - 1)
    def _():
        follow[...] = jnp.zeros_like(follow)

    @pl.when(me == 0)
    def _():
        arrive[...] = jnp.zeros_like(arrive)

    def column(s):
        g = jnp.concatenate([sig_ref[0, s], jnp.zeros((6, sig_ref.shape[-1]), F32)], axis=0).T
        return g[:, 0:1], g[:, 1:2]

    sig = [column(s) for s in range(2)]

    def store(ref, re, im):
        ref[...] = jnp.concatenate([re.astype(BF16), im.astype(BF16)], axis=1)

    def cprod(mr, mi, rhs):
        x = dot(mr, rhs)
        y = dot(mi, rhs)
        return x[:, :h] - y[:, h:], x[:, h:] + y[:, :h]

    def cprod_adj(mr, mi, rhs):
        x = dot(mr, rhs)
        y = dot(mi, rhs)
        return x[:, :h] + y[:, h:], x[:, h:] - y[:, :h]

    def local(s):
        x = st[s].astype(F32)
        xr, xi = x[:, :h], x[:, h:]
        gr, gi = sig[s]
        return (src[s, 0] + (gr * xr - gi * xi), src[s, 1] + (gr * xi + gi * xr))

    def sends(sweep):
        to_prev = pltpu.make_async_remote_copy(
            src_ref=st.at[0], dst_ref=follow.at[sweep],
            send_sem=send_sem.at[0, sweep], recv_sem=recv_sem.at[0, sweep],
            device_id=(en, prev), device_id_type=MESH)
        to_next = pltpu.make_async_remote_copy(
            src_ref=hand.at[sweep], dst_ref=arrive.at[sweep],
            send_sem=send_sem.at[1, sweep], recv_sem=recv_sem.at[1, sweep],
            device_id=(en, nxt), device_id_type=MESH)
        return to_prev, to_next

    sweeps = SWEEPS - 1
    copies = [sends(sweep) for sweep in range(sweeps)]

    loads[0].wait()
    for s in range(2):
        loads[1 + s].wait()
        rhs = jnp.concatenate([src[s, 0].astype(BF16), src[s, 1].astype(BF16)], axis=1)
        re, im = cprod(pre[s, 0], pre[s, 1], rhs)
        store(st.at[s], re, im)
        if s == 0:
            @pl.when(me > 0)
            def _():
                copies[0][0].start()

    for s in range(2):
        loads[3 + s].wait()
        for p in range(2):
            ct[s, p] = cpl[s, p].T

    for sweep in range(sweeps):
        to_prev, to_next = copies[sweep]
        hr, hi = cprod_adj(ct[1, 0], ct[1, 1], st[1])
        store(hand.at[sweep], hr, hi)

        @pl.when(me < n - 1)
        def _():
            to_next.start()

        lr, li = cprod_adj(ct[0, 0], ct[0, 1], st[0])
        lr = lr.astype(BF16).astype(F32)
        li = li.astype(BF16).astype(F32)
        a1r, a1i = local(1)
        ur, ui = cprod(cpl[0, 0], cpl[0, 1], st[1])
        a0r, a0i = local(0)

        @pl.when(me > 0)
        def _():
            to_next.wait_recv()

        x = arrive[sweep].astype(F32)
        d0 = jnp.concatenate([((a0r + ur) + x[:, :h]).astype(BF16),
                              ((a0i + ui) + x[:, h:]).astype(BF16)], axis=1)

        @pl.when(me > 0)
        def _():
            to_prev.wait_send()

        n0r, n0i = cprod(pre[0, 0], pre[0, 1], d0)
        store(st.at[0], n0r, n0i)
        if sweep + 1 < sweeps:
            @pl.when(me > 0)
            def _():
                copies[sweep + 1][0].start()

        @pl.when(me < n - 1)
        def _():
            to_prev.wait_recv()

        fr, fi = cprod(cpl[1, 0], cpl[1, 1], follow[sweep])
        d1 = jnp.concatenate([((a1r + fr) + lr).astype(BF16),
                              ((a1i + fi) + li).astype(BF16)], axis=1)
        n1r, n1i = cprod(pre[1, 0], pre[1, 1], d1)
        store(st.at[1], n1r, n1i)

        @pl.when(me < n - 1)
        def _():
            to_next.wait_send()

    swap = pltpu.make_async_remote_copy(
        src_ref=st, dst_ref=other, send_sem=swap_sem.at[0], recv_sem=swap_sem.at[1],
        device_id=(mate, me), device_id_type=MESH)
    swap.start()
    out_ref[0] = st[...]
    swap.wait()
    out_ref[1] = other[...]


def solve(precond, coupling, source, sigma, n):
    m, h = source.shape[-2:]
    sweeps = SWEEPS - 1
    half = (m, 2 * h)
    vmem = pl.BlockSpec(memory_space=pltpu.VMEM)
    anyspace = pl.BlockSpec(memory_space=pl.ANY)
    return pl.pallas_call(
        functools.partial(solve_kernel, n),
        out_shape=jax.ShapeDtypeStruct((2, 2) + half, BF16),
        in_specs=[anyspace, anyspace, anyspace, vmem],
        out_specs=vmem,
        scratch_shapes=[
            pltpu.VMEM(precond.shape[1:], BF16),
            pltpu.VMEM(coupling.shape, BF16),
            pltpu.VMEM(source.shape[1:], F32),
            pltpu.VMEM(coupling.shape, BF16),
            pltpu.VMEM((2,) + half, BF16),
            pltpu.VMEM((sweeps,) + half, BF16),
            pltpu.VMEM((sweeps,) + half, BF16),
            pltpu.VMEM((sweeps,) + half, BF16),
            pltpu.VMEM((2,) + half, BF16),
            pltpu.SemaphoreType.DMA((5,)),
            pltpu.SemaphoreType.DMA((2, sweeps)),
            pltpu.SemaphoreType.DMA((2, sweeps)),
            pltpu.SemaphoreType.DMA((2,)),
        ],
        compiler_params=pltpu.CompilerParams(collective_id=0, has_side_effects=True),
    )(precond, coupling, source, sigma)


def nt_dot(a, b):
    return lax.dot_general(a, b, (((1,), (1,)), ((), ())), preferred_element_type=F32)


def self_kernel(both_ref, scale_ref, less_ref, great_ref):
    h = both_ref.shape[-1] // 2
    for s in range(2):
        own = both_ref[0, s]
        mate = both_ref[1, s]
        a = jnp.concatenate([own, mate], axis=1)
        swapped = jnp.concatenate([own[:, h:], -own[:, :h], mate[:, h:], -mate[:, :h]], axis=1)
        af = a.astype(F32)
        for q, out in enumerate((less_ref, great_ref)):
            b = (af * scale_ref[q]).astype(BF16)
            out[0, s, 0] = nt_dot(a, b).astype(BF16)
            out[0, s, 1] = nt_dot(swapped, b).astype(BF16)


def self_energy(both, scales):
    m = both.shape[2]
    vmem = pl.BlockSpec(memory_space=pltpu.VMEM)
    shape = jax.ShapeDtypeStruct((1, 2, 2, m, m), BF16)
    return pl.pallas_call(
        self_kernel,
        out_shape=(shape, shape),
        in_specs=[vmem, vmem],
        out_specs=(vmem, vmem),
    )(both, scales)


def body(precond, coupling, source, sigma_ret, occupation, shift_offsets, shift_weights):
    n = lax.axis_size("space")
    mode_count = source.shape[-1]
    energy_total = occupation.shape[0]
    both = solve(precond, coupling, source, sigma_ret, n)
    e = lax.axis_index("energy")
    offsets = lax.dynamic_index_in_dim(shift_offsets, e, 0, keepdims=False)
    weights_here = lax.dynamic_index_in_dim(shift_weights, e, 0, keepdims=False)
    targets = e + offsets
    inside = (targets >= 0) & (targets < energy_total)
    weights = jnp.where(inside, weights_here, jnp.zeros_like(weights_here)) / mode_count
    coef_own = jnp.sum(jnp.where(targets == e, weights, 0.0))
    coef_other = jnp.sum(jnp.where(targets == 1 - e, weights, 0.0))
    occ_own = lax.dynamic_index_in_dim(occupation, e, 0, keepdims=False)
    occ_other = lax.dynamic_index_in_dim(occupation, 1 - e, 0, keepdims=False)
    less = jnp.concatenate([coef_own * occ_own] * 2 + [coef_other * occ_other] * 2)
    great = jnp.concatenate([coef_own * (1.0 - occ_own)] * 2 + [coef_other * (1.0 - occ_other)] * 2)
    scales = jnp.stack([less, great])[:, None, :]
    return self_energy(both, scales)


def solution(mesh):
    placed = (
        P("energy", "space", None, None, None),
        P("space", None, None, None),
        P("energy", "space", None, None, None),
        P("energy", "space", None, None),
        P(),
        P(),
        P(),
    )
    return jax.shard_map(
        body,
        mesh=mesh,
        in_specs=placed,
        out_specs=(P("energy", "space", None, None, None), P("energy", "space", None, None, None)),
        check_vma=False,
    )
```

time: 58.3 us -> 50.1 us (0.86)
  local copies, waits for them, and re-layouts: 4.96 us -> 0.59 us
  matrix products: 3.78 us -> 0 us
  Pallas kernels: 41.6 us -> 45.2 us
  starting transfers between devices: 3.1 us -> 0 us
    pallas_call x0 -> x1, Pallas kernels: none -> 5.08 us  [self_energy(): pl.pallas_call(self_kernel, out_shape=(shape, shape), in_specs=[vmem, vme...]
    dot_general x8 -> x0, matrix products: 3.78 us -> none  [the longest x4 1.9 us: self_energy(): real_part = ein(pr, br) + ein(pi, bi)]
    ppermute x1 -> x0, starting transfers between devices: 3.1 us -> none  [body(): other = lax.ppermute(own, 'energy', [(0, 1), (1, 0)])]
    unnamed x10 -> x0, local copies, waits for them, and re-layouts: 2.92 us -> none
    pallas_call x1, Pallas kernels: 41.6 us -> 40.1 us  [solve(): pl.pallas_call(functools.partial(solve_kernel, n), out_shape=jax.ShapeDty...]
    broadcast_in_dim x1, local copies, waits for them, and re-layouts: 2.04 us -> 0.59 us  [body(): scales = jnp.stack([less, great])[:, None, :]]
    squeeze x1 -> x0, other arithmetic: 1.15 us -> none  [self_energy(): pr, pi = (picked[:, 0], picked[:, 1])]
    mul x1, other arithmetic: 1.3 us -> 2.06 us  [body(): coef_own * occ_own]
  transfers between devices with their start and end apart: 1 -> 0, of which waited for: 0 -> 0; matrix products, arithmetic and copies ran while one was open for 3% -> 0% of each run, Pallas kernels for 0% -> 0%
where the time goes in v2:
time: 50.1 us; the launch traced here: 49.9 us
  Pallas kernels  45.2 us (90%)
  other arithmetic  3.4 us (7%)
  between operations  0.65 us (1%)
  local copies, waits for them, and re-layouts  0.59 us (1%)
    pallas_call x1, Pallas kernels, solve(): pl.pallas_call(functools.partial(solve_kernel, n), out_shape=jax.ShapeDty...  40.1 us
    pallas_call x1, Pallas kernels, self_energy(): pl.pallas_call(self_kernel, out_shape=(shape, shape), in_specs=[vmem, vme...  5.08 us
    mul x1, other arithmetic, body(): coef_own * occ_own  2.06 us
    reduce_sum x1, other arithmetic, body(): coef_own = jnp.sum(jnp.where(targets == e, weights, 0.0))  1.32 us

profile of v2, /device:TPU:129, one launch (start us, length us, event | category | flops | bytes accessed | tf_op | source)
XLA Modules:
  0.0 49.9 jit_solution(3672340011030589156)
XLA Ops:
  0.6 1.3 %fusion.1 = (f32[]{:T(128)}, f32[]{:T(128)}) fusion(s32[]{:T(128)S(6)} %axis_index.15, f32[2,4]{1,0:T(2,128)} %param.13, s32[]{:T(128)S(6)} %select_n.25, s32[2,4]{1,0:T(2,128)} %param.12, s32[]{:T(128)S(6)} %sub.12), kind=kLoop, calls=%fused_computation.11 | loop fusion | flops 46 | bytes 52 | tf_op jit(solution)/shard_map/reduce_sum | solution.py:233
  2.0 2.1 %multiply_bitcast_fusion.3 = (f32[128]{0:T(128)S(1)}, f32[128]{0:T(128)S(1)}, f32[128]{0:T(128)S(1)}, f32[128]{0:T(128)S(1)}) fusion(f32[]{:T(128)} %get-tuple-element.2, f32[2,128]{1,0:T(2,128)} %param.11, s32[]{:T(128)S(6)} %select_n.25, s32[]{:T(128)S(6)} %select_n.30, f32[]{:T(128)} %get-tuple-element.3), kind=kLoop, calls=%fused_computation.16 | loop fusion | flops 768 | bytes 3088 | tf_op jit(solution)/shard_map/mul | solution.py:237
  4.0 0.6 %broadcast_in_dim.6.scale_ref = f32[2,1,512]{2,1,0:T(1,128)} reshape(f32[2,512]{1,0:T(2,128)S(1)} %pad_maximum_fusion) | data formatting | bytes 8192 | tf_op jit(solution)/shard_map/broadcast_in_dim | solution.py:239
  4.6 40.1 %shard_map.86.both_ref = bf16[2,2,512,256]{3,2,1,0:T(8,128)(2,1)} custom-call(bf16[1,2,2,512,512]{4,3,2,1,0:T(8,128)(2,1)} %pre_hbm.1, bf16[2,2,512,512]{3,2,1,0:T(8,128)(2,1)} %cpl_hbm.1, f32[1,2,2,512,128]{4,3,2,1,0:T(8,128)} %src_hbm.1, f32[1,2,2,512]{3,2,1,0:T(2,128)} %sig_ref.1), custom_call_target="tpu_custom_call" | custom-call | tf_op jit(solution)/shard_map/pallas_call | solution.py:168
  44.8 5.1 %shard_map.87 = (bf16[1,2,2,512,512]{4,3,2,1,0:T(8,128)(2,1)}, bf16[1,2,2,512,512]{4,3,2,1,0:T(8,128)(2,1)}) custom-call(bf16[2,2,512,256]{3,2,1,0:T(8,128)(2,1)} %shard_map.86.both_ref, f32[2,1,512]{2,1,0:T(1,128)} %broadcast_in_dim.6.scale_ref), custom_call_target="tpu_custom_call" | custom-call | tf_op jit(solution)/shard_map/pallas_call | solution.py:214
  (2 shorter events, 0.0 us)

commit v3 on v2

--- a/solution.py
+++ b/solution.py
@@ -193,51 +193,61 @@
     return lax.dot_general(a, b, (((1,), (1,)), ((), ())), preferred_element_type=F32)
 
 
-def self_kernel(both_ref, scale_ref, less_ref, great_ref):
+def self_kernel(both_ref, occ_ref, off_ref, wt_ref, less_ref, great_ref):
     h = both_ref.shape[-1] // 2
-    for s in range(2):
-        own = both_ref[0, s]
-        mate = both_ref[1, s]
-        a = jnp.concatenate([own, mate], axis=1)
-        swapped = jnp.concatenate([own[:, h:], -own[:, :h], mate[:, h:], -mate[:, :h]], axis=1)
-        af = a.astype(F32)
-        for q, out in enumerate((less_ref, great_ref)):
-            b = (af * scale_ref[q]).astype(BF16)
-            out[0, s, 0] = nt_dot(a, b).astype(BF16)
-            out[0, s, 1] = nt_dot(swapped, b).astype(BF16)
-
-
-def self_energy(both, scales):
-    m = both.shape[2]
-    vmem = pl.BlockSpec(memory_space=pltpu.VMEM)
+    energy_total = occ_ref.shape[0]
+    e = lax.axis_index("energy")
+    mate = 1 - e
+    coef_own = jnp.float32(0.0)
+    coef_mate = jnp.float32(0.0)
+    for j in range(off_ref.shape[1]):
+        t = e + off_ref[e, j]
+        inside = jnp.logical_and(t >= 0, t < energy_total)
+        w = jnp.where(inside, wt_ref[e, j], jnp.float32(0.0)) / h
+        coef_own = coef_own + jnp.where(t == e, w, jnp.float32(0.0))
+        coef_mate = coef_mate + jnp.where(t == mate, w, jnp.float32(0.0))
+    occ_own = occ_ref[pl.ds(e, 1), :]
+    occ_mate = occ_ref[pl.ds(mate, 1), :]
+    scales = []
+    for own_part, mate_part in ((occ_own, occ_mate), (1.0 - occ_own, 1.0 - occ_mate)):
+        so = coef_own * own_part
+        sm = coef_mate * mate_part
+        scales.append(jnp.concatenate([so, so, sm, sm], axis=1))
+    own = both_ref[0, 0]
+    mate_states = both_ref[1, 0]
+    a = jnp.concatenate([own, mate_states], axis=1)
+    swapped = jnp.concatenate(
+        [own[:, h:], -own[:, :h], mate_states[:, h:], -mate_states[:, :h]], axis=1)
+    af = a.astype(F32)
+    for scale, out in zip(scales, (less_ref, great_ref)):
+        b = (af * scale).astype(BF16)
+        out[0, 0, 0] = nt_dot(a, b).astype(BF16)
+        out[0, 0, 1] = nt_dot(swapped, b).astype(BF16)
+
+
+def self_energy(both, occupation, shift_offsets, shift_weights):
+    m, w = both.shape[2:]
     shape = jax.ShapeDtypeStruct((1, 2, 2, m, m), BF16)
+    smem = pl.BlockSpec(memory_space=pltpu.SMEM)
+    out_spec = pl.BlockSpec((1, 1, 2, m, m), lambda s: (0, s, 0, 0, 0))
     return pl.pallas_call(
         self_kernel,
         out_shape=(shape, shape),
-        in_specs=[vmem, vmem],
-        out_specs=(vmem, vmem),
-    )(both, scales)
+        grid=(2,),
+        in_specs=[
+            pl.BlockSpec((2, 1, m, w), lambda s: (0, s, 0, 0)),
+            pl.BlockSpec(occupation.shape, lambda s: (0, 0)),
+            smem,
+            smem,
+        ],
+        out_specs=(out_spec, out_spec),
+    )(both, occupation, shift_offsets, shift_weights)
 
 
 def body(precond, coupling, source, sigma_ret, occupation, shift_offsets, shift_weights):
     n = lax.axis_size("space")
-    mode_count = source.shape[-1]
-    energy_total = occupation.shape[0]
     both = solve(precond, coupling, source, sigma_ret, n)
-    e = lax.axis_index("energy")
-    offsets = lax.dynamic_index_in_dim(shift_offsets, e, 0, keepdims=False)
-    weights_here = lax.dynamic_index_in_dim(shift_weights, e, 0, keepdims=False)
-    targets = e + offsets
-    inside = (targets >= 0) & (targets < energy_total)
-    weights = jnp.where(inside, weights_here, jnp.zeros_like(weights_here)) / mode_count
-    coef_own = jnp.sum(jnp.where(targets == e, weights, 0.0))
-    coef_other = jnp.sum(jnp.where(targets == 1 - e, weights, 0.0))
-    occ_own = lax.dynamic_index_in_dim(occupation, e, 0, keepdims=False)
-    occ_other = lax.dynamic_index_in_dim(occupation, 1 - e, 0, keepdims=False)
-    less = jnp.concatenate([coef_own * occ_own] * 2 + [coef_other * occ_other] * 2)
-    great = jnp.concatenate([coef_own * (1.0 - occ_own)] * 2 + [coef_other * (1.0 - occ_other)] * 2)
-    scales = jnp.stack([less, great])[:, None, :]
-    return self_energy(both, scales)
+    return self_energy(both, occupation, shift_offsets, shift_weights)
 
 
 def solution(mesh):

time: 50.1 us -> 45.8 us (0.914)
  other arithmetic: 3.4 us -> 0 us
  local copies, waits for them, and re-layouts: 0.59 us -> 0 us
    mul x1 -> x0, other arithmetic: 2.06 us -> none  [body(): coef_own * occ_own]
    reduce_sum x1 -> x0, other arithmetic: 1.32 us -> none  [body(): coef_own = jnp.sum(jnp.where(targets == e, weights, 0.0))]
    broadcast_in_dim x1 -> x0, local copies, waits for them, and re-layouts: 0.59 us -> none  [body(): scales = jnp.stack([less, great])[:, None, :]]
where the time goes in v3:
time: 45.8 us; the launch traced here: 45.6 us
  Pallas kernels  45 us (98%)
  between operations  0.64 us (1%)
    pallas_call x1, Pallas kernels, solve(): pl.pallas_call(functools.partial(solve_kernel, n), out_shape=jax.ShapeDty...  40.3 us
    pallas_call x1, Pallas kernels, self_energy(): pl.pallas_call(self_kernel, out_shape=(shape, shape), grid=(2,), in_specs...  4.73 us

profile of v3, /device:TPU:129, one launch (start us, length us, event | category | flops | bytes accessed | tf_op | source)
XLA Modules:
  0.0 45.6 jit_solution(1824223590379515178)
XLA Ops:
  0.6 40.3 %shard_map.86.both_ref = bf16[2,2,512,256]{3,2,1,0:T(8,128)(2,1)} custom-call(bf16[1,2,2,512,512]{4,3,2,1,0:T(8,128)(2,1)} %pre_hbm.1, bf16[2,2,512,512]{3,2,1,0:T(8,128)(2,1)} %cpl_hbm.1, f32[1,2,2,512,128]{4,3,2,1,0:T(8,128)} %src_hbm.1, f32[1,2,2,512]{3,2,1,0:T(2,128)} %sig_ref.1), custom_call_target="tpu_custom_call" | custom-call | tf_op jit(solution)/shard_map/pallas_call | solution.py:168
  40.9 4.7 %shard_map.87 = (bf16[1,2,2,512,512]{4,3,2,1,0:T(8,128)(2,1)}, bf16[1,2,2,512,512]{4,3,2,1,0:T(8,128)(2,1)}) custom-call(bf16[2,2,512,256]{3,2,1,0:T(8,128)(2,1)} %shard_map.86.both_ref, f32[2,128]{1,0:T(2,128)} %occ_ref.1, s32[2,4]{1,0:T(2,128)} %off_ref.1, f32[2,4]{1,0:T(2,128)} %wt_ref.1), custom_call_target="tpu_custom_call" | custom-call | tf_op jit(solution)/shard_map/pallas_call | solution.py:233

commit v4 on v3

v4 whole, which is shorter than its diff:
```python
import functools

import jax
import jax.numpy as jnp
from jax import lax
from jax.experimental import pallas as pl
from jax.experimental.pallas import tpu as pltpu
from jax.sharding import PartitionSpec as P

SWEEPS = 4
MESH = pl.DeviceIdType.MESH
F32 = jnp.float32
BF16 = jnp.bfloat16


def dot(a, b):
    return jnp.dot(a, b, preferred_element_type=F32)


def solve_kernel(n, chunks, pre_hbm, cpl_hbm, src_hbm, sig_ref, out_ref,
                 pre, cpl, src, srcc, ct, st, follow, arrive, hand, other, part,
                 load_sem, send_sem, recv_sem, swap_sem):
    me = lax.axis_index("space")
    en = lax.axis_index("energy")
    prev = lax.rem(me + n - 1, n)
    nxt = lax.rem(me + 1, n)
    mate = 1 - en
    w = st.shape[-1]
    h = w // 2

    loads = [pltpu.make_async_copy(src_hbm.at[0], src, load_sem.at[0])]
    loads += [pltpu.make_async_copy(pre_hbm.at[0, s], pre.at[s], load_sem.at[1 + s]) for s in range(2)]
    loads += [pltpu.make_async_copy(cpl_hbm.at[s], cpl.at[s], load_sem.at[3 + s]) for s in range(2)]
    for c in loads:
        c.start()

    barrier = pltpu.get_barrier_semaphore()
    for peer in ((en, prev), (en, nxt), (mate, me)):
        pl.semaphore_signal(barrier, inc=1, device_id=peer, device_id_type=MESH)
    pl.semaphore_wait(barrier, 3)

    @pl.when(me == n - 1)
    def _():
        follow[...] = jnp.zeros_like(follow)

    @pl.when(me == 0)
    def _():
        arrive[...] = jnp.zeros_like(arrive)

    lanes = lax.broadcasted_iota(jnp.int32, (1, w), 1)
    low = lanes < h
    neg_low = jnp.where(low, -1.0, 1.0).astype(F32)

    def turn(x):
        return pltpu.roll(x, h, 1)

    def column(s):
        g = jnp.concatenate([sig_ref[0, s], jnp.zeros((6, sig_ref.shape[-1]), F32)], axis=0).T
        return g[:, 0:1], g[:, 1:2]

    sig = [column(s) for s in range(2)]

    def cprod(mr, mi, rhs):
        return dot(mr, rhs) + neg_low * turn(dot(mi, rhs))

    def cprod_adj(mr, mi, rhs):
        return dot(mr, rhs) - neg_low * turn(dot(mi, rhs))

    def local(c, s):
        x = st[c, s].astype(F32)
        gr, gi = sig[s]
        return srcc[c, s] + (gr * x + (gi * neg_low) * turn(x))

    sweeps = SWEEPS - 1

    def sends(sweep, c):
        to_prev = pltpu.make_async_remote_copy(
            src_ref=st.at[c, 0], dst_ref=follow.at[sweep, c],
            send_sem=send_sem.at[0, sweep, c], recv_sem=recv_sem.at[0, sweep, c],
            device_id=(en, prev), device_id_type=MESH)
        to_next = pltpu.make_async_remote_copy(
            src_ref=hand.at[sweep, c], dst_ref=arrive.at[sweep, c],
            send_sem=send_sem.at[1, sweep, c], recv_sem=recv_sem.at[1, sweep, c],
            device_id=(en, nxt), device_id_type=MESH)
        return to_prev, to_next

    copies = [[sends(sweep, c) for c in range(chunks)] for sweep in range(sweeps)]

    loads[0].wait()
    for s in range(2):
        re = src[s, 0]
        im = src[s, 1]
        srcc[0, s] = jnp.where(low, re, turn(im))
        srcc[1, s] = jnp.where(low, turn(re), im)

    for s in range(2):
        loads[1 + s].wait()
        for c in range(chunks):
            st[c, s] = cprod(pre[s, 0], pre[s, 1], srcc[c, s].astype(BF16)).astype(BF16)
            if s == 0:
                @pl.when(me > 0)
                def _():
                    copies[0][c][0].start()

    for s in range(2):
        loads[3 + s].wait()
        for p in range(2):
            ct[s, p] = cpl[s, p].T

    def phase1(sweep, c):
        to_prev, to_next = copies[sweep][c]
        hand[sweep, c] = cprod_adj(ct[1, 0], ct[1, 1], st[c, 1]).astype(BF16)

        @pl.when(me < n - 1)
        def _():
            to_next.start()

        part[c, 2] = cprod_adj(ct[0, 0], ct[0, 1], st[c, 0]).astype(BF16).astype(F32)
        part[c, 1] = local(c, 1)
        part[c, 0] = local(c, 0) + cprod(cpl[0, 0], cpl[0, 1], st[c, 1])

    def phase2(sweep, c):
        to_prev, to_next = copies[sweep][c]

        @pl.when(me > 0)
        def _():
            to_next.wait_recv()

        d0 = (part[c, 0] + arrive[sweep, c].astype(F32)).astype(BF16)

        @pl.when(me > 0)
        def _():
            to_prev.wait_send()

        st[c, 0] = cprod(pre[0, 0], pre[0, 1], d0).astype(BF16)
        if sweep + 1 < sweeps:
            @pl.when(me > 0)
            def _():
                copies[sweep + 1][c][0].start()

        @pl.when(me < n - 1)
        def _():
            to_prev.wait_recv()

        upper = cprod(cpl[1, 0], cpl[1, 1], follow[sweep, c])
        d1 = ((part[c, 1] + upper) + part[c, 2]).astype(BF16)
        st[c, 1] = cprod(pre[1, 0], pre[1, 1], d1).astype(BF16)

        @pl.when(me < n - 1)
        def _():
            to_next.wait_send()

    swaps = [pltpu.make_async_remote_copy(
        src_ref=st.at[c], dst_ref=other.at[c], send_sem=swap_sem.at[0, c],
        recv_sem=swap_sem.at[1, c], device_id=(mate, me), device_id_type=MESH)
        for c in range(chunks)]

    for c in range(chunks):
        phase1(0, c)
    for sweep in range(sweeps):
        for c in range(chunks):
            phase2(sweep, c)
            if sweep + 1 < sweeps:
                phase1(sweep + 1, c)
            else:
                swaps[c].start()

    for c in range(chunks):
        for s in range(2):
            out_ref[0, s, :, c * w:(c + 1) * w] = st[c, s]
    for c in range(chunks):
        swaps[c].wait()
        for s in range(2):
            out_ref[1, s, :, c * w:(c + 1) * w] = other[c, s]


def solve(precond, coupling, source, sigma, n):
    m, h = source.shape[-2:]
    chunks = 2
    sweeps = SWEEPS - 1
    blk = (m, 2 * h // chunks)
    vmem = pl.BlockSpec(memory_space=pltpu.VMEM)
    anyspace = pl.BlockSpec(memory_space=pl.ANY)
    return pl.pallas_call(
        functools.partial(solve_kernel, n, chunks),
        out_shape=jax.ShapeDtypeStruct((2, 2, m, 2 * h), BF16),
        in_specs=[anyspace, anyspace, anyspace, vmem],
        out_specs=vmem,
        scratch_shapes=[
            pltpu.VMEM(precond.shape[1:], BF16),
            pltpu.VMEM(coupling.shape, BF16),
            pltpu.VMEM(source.shape[1:], F32),
            pltpu.VMEM((chunks, 2) + blk, F32),
            pltpu.VMEM(coupling.shape, BF16),
            pltpu.VMEM((chunks, 2) + blk, BF16),
            pltpu.VMEM((sweeps, chunks) + blk, BF16),
            pltpu.VMEM((sweeps, chunks) + blk, BF16),
            pltpu.VMEM((sweeps, chunks) + blk, BF16),
            pltpu.VMEM((chunks, 2) + blk, BF16),
            pltpu.VMEM((chunks, 3) + blk, F32),
            pltpu.SemaphoreType.DMA((5,)),
            pltpu.SemaphoreType.DMA((2, sweeps, chunks)),
            pltpu.SemaphoreType.DMA((2, sweeps, chunks)),
            pltpu.SemaphoreType.DMA((2, chunks)),
        ],
        compiler_params=pltpu.CompilerParams(collective_id=0, has_side_effects=True),
    )(precond, coupling, source, sigma)


def nt_dot(a, b):
    return lax.dot_general(a, b, (((1,), (1,)), ((), ())), preferred_element_type=F32)


def self_kernel(both_ref, occ_ref, off_ref, wt_ref, less_ref, great_ref):
    h = both_ref.shape[-1] // 2
    energy_total = occ_ref.shape[0]
    e = lax.axis_index("energy")
    mate = 1 - e
    coef_own = jnp.float32(0.0)
    coef_mate = jnp.float32(0.0)
    for j in range(off_ref.shape[1]):
        t = e + off_ref[e, j]
        inside = jnp.logical_and(t >= 0, t < energy_total)
        w = jnp.where(inside, wt_ref[e, j], jnp.float32(0.0)) / h
        coef_own = coef_own + jnp.where(t == e, w, jnp.float32(0.0))
        coef_mate = coef_mate + jnp.where(t == mate, w, jnp.float32(0.0))
    occ_own = occ_ref[pl.ds(e, 1), :]
    occ_mate = occ_ref[pl.ds(mate, 1), :]
    lanes = lax.broadcasted_iota(jnp.int32, (1, h), 1)
    low = lanes < h // 2
    pos_low = jnp.where(low, 1.0, -1.0).astype(BF16)

    def turn(x):
        return pltpu.roll(x, h // 2, 1)

    def spread(v):
        return jnp.concatenate([jnp.where(low, v, turn(v)), jnp.where(low, turn(v), v)], axis=1)

    scales = []
    for own_part, mate_part in ((occ_own, occ_mate), (1.0 - occ_own, 1.0 - occ_mate)):
        scales.append(jnp.concatenate([spread(coef_own * own_part), spread(coef_mate * mate_part)], axis=1))
    own = both_ref[0, 0]
    mate_states = both_ref[1, 0]
    a = jnp.concatenate([own, mate_states], axis=1)
    blocks = [x[:, i * h:(i + 1) * h] for x in (own, mate_states) for i in range(2)]
    swapped = jnp.concatenate(
        [(turn(b.astype(F32)) * pos_low.astype(F32)).astype(BF16) for b in blocks], axis=1)
    af = a.astype(F32)
    for scale, out in zip(scales, (less_ref, great_ref)):
        b = (af * scale).astype(BF16)
        out[0, 0, 0] = nt_dot(a, b).astype(BF16)
        out[0, 0, 1] = nt_dot(swapped, b).astype(BF16)


def self_energy(both, occupation, shift_offsets, shift_weights):
    m, w = both.shape[2:]
    shape = jax.ShapeDtypeStruct((1, 2, 2, m, m), BF16)
    smem = pl.BlockSpec(memory_space=pltpu.SMEM)
    out_spec = pl.BlockSpec((1, 1, 2, m, m), lambda s: (0, s, 0, 0, 0))
    return pl.pallas_call(
        self_kernel,
        out_shape=(shape, shape),
        grid=(2,),
        in_specs=[
            pl.BlockSpec((2, 1, m, w), lambda s: (0, s, 0, 0)),
            pl.BlockSpec(occupation.shape, lambda s: (0, 0)),
            smem,
            smem,
        ],
        out_specs=(out_spec, out_spec),
    )(both, occupation, shift_offsets, shift_weights)


def body(precond, coupling, source, sigma_ret, occupation, shift_offsets, shift_weights):
    n = lax.axis_size("space")
    both = solve(precond, coupling, source, sigma_ret, n)
    return self_energy(both, occupation, shift_offsets, shift_weights)


def solution(mesh):
    placed = (
        P("energy", "space", None, None, None),
        P("space", None, None, None),
        P("energy", "space", None, None, None),
        P("energy", "space", None, None),
        P(),
        P(),
        P(),
    )
    return jax.shard_map(
        body,
        mesh=mesh,
        in_specs=placed,
        out_specs=(P("energy", "space", None, None, None), P("energy", "space", None, None, None)),
        check_vma=False,
    )
```

time: 45.8 us -> 45.4 us (level)
    pallas_call x1, Pallas kernels: 40.3 us -> 39.8 us  [solve(): pl.pallas_call(functools.partial(solve_kernel, n, chunks), out_shape=jax....]
where the time goes in v4:
time: 45.4 us; the launch traced here: 45.3 us
  Pallas kernels  44.7 us (98%)
  between operations  0.64 us (1%)
    pallas_call x1, Pallas kernels, solve(): pl.pallas_call(functools.partial(solve_kernel, n, chunks), out_shape=jax....  39.8 us
    pallas_call x1, Pallas kernels, self_energy(): pl.pallas_call(self_kernel, out_shape=(shape, shape), grid=(2,), in_specs...  4.88 us

profile of v4, /device:TPU:129, one launch (start us, length us, event | category | flops | bytes accessed | tf_op | source)
XLA Modules:
  0.0 45.3 jit_solution(8069311115578713247)
XLA Ops:
  0.6 39.8 %shard_map.86.both_ref = bf16[2,2,512,256]{3,2,1,0:T(8,128)(2,1)} custom-call(bf16[1,2,2,512,512]{4,3,2,1,0:T(8,128)(2,1)} %pre_hbm.1, bf16[2,2,512,512]{3,2,1,0:T(8,128)(2,1)} %cpl_hbm.1, f32[1,2,2,512,128]{4,3,2,1,0:T(8,128)} %src_hbm.1, f32[1,2,2,512]{3,2,1,0:T(2,128)} %sig_ref.1), custom_call_target="tpu_custom_call" | custom-call | tf_op jit(solution)/shard_map/pallas_call | solution.py:184
  40.4 4.9 %shard_map.87 = (bf16[1,2,2,512,512]{4,3,2,1,0:T(8,128)(2,1)}, bf16[1,2,2,512,512]{4,3,2,1,0:T(8,128)(2,1)}) custom-call(bf16[2,2,512,256]{3,2,1,0:T(8,128)(2,1)} %shard_map.86.both_ref, f32[2,128]{1,0:T(2,128)} %occ_ref.1, s32[2,4]{1,0:T(2,128)} %off_ref.1, f32[2,4]{1,0:T(2,128)} %wt_ref.1), custom_call_target="tpu_custom_call" | custom-call | tf_op jit(solution)/shard_map/pallas_call | solution.py:260

commit v5 on v3

v5 whole, which is shorter than its diff:
```python
import functools

import jax
import jax.numpy as jnp
from jax import lax
from jax.experimental import pallas as pl
from jax.experimental.pallas import tpu as pltpu
from jax.sharding import PartitionSpec as P

SWEEPS = 4
MESH = pl.DeviceIdType.MESH
F32 = jnp.float32
BF16 = jnp.bfloat16


def dot(a, b):
    return jnp.dot(a, b, preferred_element_type=F32)


def exchange_kernel(n, st0_ref, hand_ref, follow_ref, arrive_ref, fbuf, abuf, send_sem, recv_sem):
    me = lax.axis_index("space")
    en = lax.axis_index("energy")
    prev = lax.rem(me + n - 1, n)
    nxt = lax.rem(me + 1, n)
    barrier = pltpu.get_barrier_semaphore()
    for peer in (prev, nxt):
        pl.semaphore_signal(barrier, inc=1, device_id=(en, peer), device_id_type=MESH)
    pl.semaphore_wait(barrier, 2)
    to_prev = pltpu.make_async_remote_copy(
        src_ref=st0_ref, dst_ref=fbuf, send_sem=send_sem.at[0], recv_sem=recv_sem.at[0],
        device_id=(en, prev), device_id_type=MESH)
    to_next = pltpu.make_async_remote_copy(
        src_ref=hand_ref, dst_ref=abuf, send_sem=send_sem.at[1], recv_sem=recv_sem.at[1],
        device_id=(en, nxt), device_id_type=MESH)

    @pl.when(me > 0)
    def _():
        to_prev.start()

    @pl.when(me < n - 1)
    def _():
        to_next.start()

    @pl.when(me < n - 1)
    def _():
        to_prev.wait_recv()
        follow_ref[...] = fbuf[...]

    @pl.when(me == n - 1)
    def _():
        follow_ref[...] = jnp.zeros_like(follow_ref)

    @pl.when(me > 0)
    def _():
        to_next.wait_recv()
        arrive_ref[...] = abuf[...]

    @pl.when(me == 0)
    def _():
        arrive_ref[...] = jnp.zeros_like(arrive_ref)

    @pl.when(me > 0)
    def _():
        to_prev.wait_send()

    @pl.when(me < n - 1)
    def _():
        to_next.wait_send()


def exchange(st0, hand, n, sweep):
    vmem = pl.BlockSpec(memory_space=pltpu.VMEM)
    shape = jax.ShapeDtypeStruct(st0.shape, BF16)
    return pl.pallas_call(
        functools.partial(exchange_kernel, n),
        out_shape=(shape, shape),
        in_specs=[vmem, vmem],
        out_specs=(vmem, vmem),
        scratch_shapes=[
            pltpu.VMEM(st0.shape, BF16),
            pltpu.VMEM(st0.shape, BF16),
            pltpu.SemaphoreType.DMA((2,)),
            pltpu.SemaphoreType.DMA((2,)),
        ],
        compiler_params=pltpu.CompilerParams(collective_id=sweep, has_side_effects=True),
        name=f"exchange_{sweep}",
    )(st0, hand)


def mult(a, b):
    return jnp.einsum("...mn,...nk->...mk", a, b, preferred_element_type=F32)


def mult_adj(a, b):
    return jnp.einsum("...nm,...nk->...mk", a, b, preferred_element_type=F32)


def cprod(m, s):
    re = mult(m[..., 0, :, :], s[..., 0, :, :]) - mult(m[..., 1, :, :], s[..., 1, :, :])
    im = mult(m[..., 0, :, :], s[..., 1, :, :]) + mult(m[..., 1, :, :], s[..., 0, :, :])
    return jnp.stack([re, im], axis=-3)


def cprod_adj(m, s):
    re = mult_adj(m[..., 0, :, :], s[..., 0, :, :]) + mult_adj(m[..., 1, :, :], s[..., 1, :, :])
    im = mult_adj(m[..., 0, :, :], s[..., 1, :, :]) - mult_adj(m[..., 1, :, :], s[..., 0, :, :])
    return jnp.stack([re, im], axis=-3)


def solve(precond, coupling, source, sigma_ret, n):
    pre = precond[0]
    src = source[0]
    states = cprod(pre, src.astype(BF16)).astype(BF16)
    sig_r = sigma_ret[0, :, 0, :, None]
    sig_i = sigma_ret[0, :, 1, :, None]
    for sweep in range(SWEEPS - 1):
        hand = cprod_adj(coupling[1], states[1]).astype(BF16)
        follow, arrive = exchange(states[0], hand, n, sweep)
        beyond = jnp.stack([states[1], follow])
        upper = cprod(coupling, beyond)
        lower = jnp.stack([arrive, cprod_adj(coupling[0], states[0]).astype(BF16)])
        xr = states[:, 0].astype(F32)
        xi = states[:, 1].astype(F32)
        local = jnp.stack([sig_r * xr - sig_i * xi, sig_r * xi + sig_i * xr], axis=1)
        driven = (src + local + upper + lower.astype(F32)).astype(BF16)
        states = cprod(pre, driven).astype(BF16)
    own = jnp.concatenate([states[:, 0], states[:, 1]], axis=-1)
    other = lax.ppermute(own, "energy", [(0, 1), (1, 0)])
    return jnp.stack([own, other])


def nt_dot(a, b):
    return lax.dot_general(a, b, (((1,), (1,)), ((), ())), preferred_element_type=F32)


def self_kernel(both_ref, occ_ref, off_ref, wt_ref, less_ref, great_ref):
    h = both_ref.shape[-1] // 2
    energy_total = occ_ref.shape[0]
    e = lax.axis_index("energy")
    mate = 1 - e
    coef_own = jnp.float32(0.0)
    coef_mate = jnp.float32(0.0)
    for j in range(off_ref.shape[1]):
        t = e + off_ref[e, j]
        inside = jnp.logical_and(t >= 0, t < energy_total)
        w = jnp.where(inside, wt_ref[e, j], jnp.float32(0.0)) / h
        coef_own = coef_own + jnp.where(t == e, w, jnp.float32(0.0))
        coef_mate = coef_mate + jnp.where(t == mate, w, jnp.float32(0.0))
    occ_own = occ_ref[pl.ds(e, 1), :]
    occ_mate = occ_ref[pl.ds(mate, 1), :]
    scales = []
    for own_part, mate_part in ((occ_own, occ_mate), (1.0 - occ_own, 1.0 - occ_mate)):
        so = coef_own * own_part
        sm = coef_mate * mate_part
        scales.append(jnp.concatenate([so, so, sm, sm], axis=1))
    own = both_ref[0, 0]
    mate_states = both_ref[1, 0]
    a = jnp.concatenate([own, mate_states], axis=1)
    swapped = jnp.concatenate(
        [own[:, h:], -own[:, :h], mate_states[:, h:], -mate_states[:, :h]], axis=1)
    af = a.astype(F32)
    for scale, out in zip(scales, (less_ref, great_ref)):
        b = (af * scale).astype(BF16)
        out[0, 0, 0] = nt_dot(a, b).astype(BF16)
        out[0, 0, 1] = nt_dot(swapped, b).astype(BF16)


def self_energy(both, occupation, shift_offsets, shift_weights):
    m, w = both.shape[2:]
    shape = jax.ShapeDtypeStruct((1, 2, 2, m, m), BF16)
    smem = pl.BlockSpec(memory_space=pltpu.SMEM)
    out_spec = pl.BlockSpec((1, 1, 2, m, m), lambda s: (0, s, 0, 0, 0))
    return pl.pallas_call(
        self_kernel,
        out_shape=(shape, shape),
        grid=(2,),
        in_specs=[
            pl.BlockSpec((2, 1, m, w), lambda s: (0, s, 0, 0)),
            pl.BlockSpec(occupation.shape, lambda s: (0, 0)),
            smem,
            smem,
        ],
        out_specs=(out_spec, out_spec),
    )(both, occupation, shift_offsets, shift_weights)


def body(precond, coupling, source, sigma_ret, occupation, shift_offsets, shift_weights):
    n = lax.axis_size("space")
    both = solve(precond, coupling, source, sigma_ret, n)
    return self_energy(both, occupation, shift_offsets, shift_weights)


def solution(mesh):
    placed = (
        P("energy", "space", None, None, None),
        P("space", None, None, None),
        P("energy", "space", None, None, None),
        P("energy", "space", None, None),
        P(),
        P(),
        P(),
    )
    return jax.shard_map(
        body,
        mesh=mesh,
        in_specs=placed,
        out_specs=(P("energy", "space", None, None, None), P("energy", "space", None, None, None)),
        check_vma=False,
    )
```

time: 45.8 us -> 98.2 us (2.14)
  matrix products: 0 us -> 29.4 us
  local copies, waits for them, and re-layouts: 0 us -> 8.55 us
  other arithmetic: 0 us -> 7.7 us
  starting transfers between devices: 0 us -> 3.71 us
  waiting for transfers between devices: 0 us -> 1.54 us
    dot_general x0 -> x52, matrix products: none -> 29.4 us  [the longest x28 18.2 us: mult(): return jnp.einsum('...mn,...nk->...mk', a, b, preferred_element_type=F32)]
    unnamed x0 -> x60, local copies, waits for them, and re-layouts: none -> 8.54 us
    another operation x0 -> x8, other arithmetic: none -> 5.78 us  [the longest x3 2.45 us: cprod(): return jnp.stack([re, im], axis=-3)]
    ppermute x0 -> x1, starting transfers between devices: none -> 3.71 us  [solve(): other = lax.ppermute(own, 'energy', [(0, 1), (1, 0)])]
    convert_element_type x0 -> x4, other arithmetic: none -> 1.92 us  [the longest x1 1.3 us: solve(): states = cprod(pre, src.astype(BF16)).astype(BF16)]
    ppermute x0 -> x1, waiting for transfers between devices: none -> 1.54 us  [solve(): other = lax.ppermute(own, 'energy', [(0, 1), (1, 0)])]
    pallas_call x1 -> x3, Pallas kernels: 40.3 us -> 40.7 us  [exchange(): pl.pallas_call(functools.partial(exchange_kernel, n), out_shape=(shape, s...]
  transfers between devices with their start and end apart: 0 -> 1, of which waited for: 0 -> 1; matrix products, arithmetic and copies ran while one was open for 0% -> 0% of each run, Pallas kernels for 0% -> 0%
where the time goes in v5:
time: 98.2 us; the launch traced here: 97.6 us
  Pallas kernels  45.5 us (46%)
  matrix products  29.4 us (30%)
  local copies, waits for them, and re-layouts  8.55 us (9%)
  other arithmetic  7.7 us (8%)
  starting transfers between devices  3.71 us (4%)
  waiting for transfers between devices  1.54 us (2%)
  between operations  1.21 us (1%)
    pallas_call x3, Pallas kernels, exchange(): pl.pallas_call(functools.partial(exchange_kernel, n), out_shape=(shape, s...  40.7 us
    dot_general x28, matrix products, mult(): return jnp.einsum('...mn,...nk->...mk', a, b, preferred_element_type=F32)  18.2 us
    dot_general x24, matrix products, mult_adj(): return jnp.einsum('...nm,...nk->...mk', a, b, preferred_element_type=F32)  11.2 us
    unnamed x60, local copies, waits for them, and re-layouts  8.54 us
    pallas_call x1, Pallas kernels, self_energy(): pl.pallas_call(self_kernel, out_shape=(shape, shape), grid=(2,), in_specs...  4.71 us
    ppermute x1, starting transfers between devices, solve(): other = lax.ppermute(own, 'energy', [(0, 1), (1, 0)])  3.71 us
    another operation x3, other arithmetic, cprod(): return jnp.stack([re, im], axis=-3)  2.45 us
    another operation x3, other arithmetic, cprod_adj(): return jnp.stack([re, im], axis=-3)  2.18 us
  transfers between devices with their start and end apart: 1, of which 1 were waited for; matrix products, arithmetic and copies ran while one was open for 0% of the time, Pallas kernels for 0%

profile of v5, /device:TPU:129, one launch (start us, length us, event | category | flops | bytes accessed | tf_op | source)
XLA Modules:
  0.0 97.6 jit_solution(7941673266733592661)
XLA Ops:
  0.6 1.3 %bitcast_convert_fusion = bf16[2,2,512,128]{3,2,1,0:T(8,128)(2,1)S(1)} fusion(f32[1,2,2,512,128]{4,3,2,1,0:T(8,128)} %param.9), kind=kLoop, calls=%fused_computation.100 | loop fusion | flops 262144 | bytes 1572864 | tf_op jit(solution)/shard_map/convert_element_type | solution.py:113
  1.9 1.7 %copy.238 = bf16[1,2,2,512,512]{4,3,1,2,0:T(8,128)(2,1)S(1)} copy(bf16[1,2,2,512,512]{4,3,2,1,0:T(8,128)(2,1)} %param.7) | data formatting | bytes 4194304 | tf_op args[0]
  3.7 0.4 fusion.137
  4.1 0.4 fusion.136
  4.6 0.4 fusion.6
  5.0 1.0 copy-done
  6.7 1.4 %fusion.67 = (f32[2,1,512,128]{3,2,1,0:T(8,128)}, f32[2,1,512,128]{3,2,1,0:T(8,128)}, bf16[2,512,128]{2,1,0:T(8,128)(2,1)S(1)}) fusion(f32[2,512]{1,0:T(2,128)S(1)} %get-tuple-element.33, f32[2,512]{1,0:T(2,128)S(1)} %get-tuple-element.34, bf16[2,512,128]{2,1,0:T(8,128)(2,1)S(1)} %fusion.6, f32[2,512,128]{2,1,0:T(8,128)S(1)} %fusion.137, ...), kind=kOutput, calls=%fused_computation.113 | convolution fusion | flops 135528448 | bytes 3416064 | tf_op jit(solution)/shard_map/...mn,...nk->...mk/dot_general | solution.py:91
  9.6 0.7 pad_maximum_fusion.8.hand_ref
  10.3 0.7 fusion.129
  11.0 14.5 %exchange_0.1 = (bf16[2,512,128]{2,1,0:T(8,128)(2,1)}, bf16[2,512,128]{2,1,0:T(8,128)(2,1)}) custom-call(bf16[2,512,128]{2,1,0:T(8,128)(2,1)} %get-tuple-element.27.st0_ref, bf16[2,512,128]{2,1,0:T(8,128)(2,1)} %pad_maximum_fusion.8.hand_ref), custom_call_target="tpu_custom_call" | custom-call | tf_op jit(solution)/shard_map/exchange_0/pallas_call | solution.py:74
  25.5 1.4 %fusion.55 = f32[2,128,512]{1,2,0:T(8,128)S(1)} fusion(bf16[2,2,512,512]{3,2,1,0:T(8,128)(2,1)S(1)} %copy-done, bf16[1,2,512,128]{3,2,1,0:T(8,128)(2,1)S(1)} %get-tuple-element.26, bf16[1,2,512,128]{3,2,1,0:T(8,128)(2,1)} %bitcast.385), kind=kOutput, calls=%fused_computation.88 | convolution fusion | flops 134742016 | bytes 2097152 | tf_op jit(solution)/shard_map/...mn,...nk->...mk/dot_general | solution.py:91
  27.0 0.4 fusion.57
  28.2 0.4 fusion.5
  28.6 0.4 fusion.4
  29.9 1.4 %copy-done.3 = bf16[1,2,2,512,512]{4,3,1,2,0:T(8,128)(2,1)S(1)} copy-done((bf16[1,2,2,512,512]{4,3,1,2,0:T(8,128)(2,1)S(1)}, bf16[1,2,2,512,512]{4,3,1,2,0:T(8,128)(2,1)}, u32[]{:S(2)}) %copy-start.3) | copy-done | bytes 2097176
  31.3 0.4 fusion.138
  31.7 0.4 fusion.8
  32.5 1.1 %fusion.85 = f32[128,512]{0,1:T(8,128)} fusion(bf16[2,2,512,512]{3,2,1,0:T(8,128)(2,1)S(1)} %copy-done, bf16[2,512,128]{2,1,0:T(8,128)(2,1)S(1)} %bitcast.370), kind=kOutput, calls=%fused_computation.144 | convolution fusion | flops 67108864 | bytes 917504 | tf_op jit(solution)/shard_map/...nm,...nk->...mk/dot_general | solution.py:95
  33.6 0.4 fusion.139
  34.0 1.4 %fusion.69 = (f32[2,1,512,128]{3,2,1,0:T(8,128)}, f32[2,1,512,128]{3,2,1,0:T(8,128)}, bf16[2,128,512]{1,2,0:T(8,128)(2,1)S(1)}) fusion(f32[2,512]{1,0:T(2,128)S(1)} %get-tuple-element.33, f32[2,512]{1,0:T(2,128)S(1)} %get-tuple-element.34, bf16[2,128,512]{1,2,0:T(8,128)(2,1)S(1)} %fusion.8, f32[2,128,512]{1,2,0:T(8,128)S(1)} %fusion.139, ...), kind=kOutput, calls=%fused_computation.115 | convolution fusion | flops 135528448 | bytes 3416064 | tf_op jit(solution)/shard_map/...mn,...nk->...mk/dot_general | solution.py:91
  35.4 1.0 %fusion.83 = f32[128,512]{0,1:T(8,128)} fusion(bf16[2,2,512,512]{3,2,1,0:T(8,128)(2,1)S(1)} %copy-done, bf16[2,512,128]{2,1,0:T(8,128)(2,1)S(1)} %bitcast.380), kind=kOutput, calls=%fused_computation.142 | convolution fusion | flops 67108864 | bytes 917504 | tf_op jit(solution)/shard_map/...nm,...nk->...mk/dot_general | solution.py:95
  37.5 0.7 pad_maximum_fusion.9.hand_ref
  38.3 0.9 fusion.126
  39.1 13.7 %exchange_1.1 = (bf16[2,512,128]{2,1,0:T(8,128)(2,1)}, bf16[2,512,128]{2,1,0:T(8,128)(2,1)}) custom-call(bf16[2,512,128]{2,1,0:T(8,128)(2,1)} %get-tuple-element.25.st0_ref, bf16[2,512,128]{2,1,0:T(8,128)(2,1)} %pad_maximum_fusion.9.hand_ref), custom_call_target="tpu_custom_call" | custom-call | tf_op jit(solution)/shard_map/exchange_1/pallas_call | solution.py:74
  52.9 1.5 %fusion.59 = f32[2,128,512]{1,2,0:T(8,128)S(1)} fusion(bf16[2,2,512,512]{3,2,1,0:T(8,128)(2,1)S(1)} %copy-done, bf16[1,2,512,128]{3,2,1,0:T(8,128)(2,1)} %get-tuple-element.24, bf16[1,2,512,128]{3,2,1,0:T(8,128)(2,1)} %bitcast.389), kind=kOutput, calls=%fused_computation.92 | convolution fusion | flops 134742016 | bytes 2097152 | tf_op jit(solution)/shard_map/...mn,...nk->...mk/dot_general | solution.py:91
  54.4 0.4 fusion.61
  55.8 0.4 fusion.3
  56.2 0.4 fusion.2
  57.2 1.4 %copy-done.4 = bf16[1,2,2,512,512]{4,3,1,2,0:T(8,128)(2,1)S(1)} copy-done((bf16[1,2,2,512,512]{4,3,1,2,0:T(8,128)(2,1)S(1)}, bf16[1,2,2,512,512]{4,3,1,2,0:T(8,128)(2,1)}, u32[]{:S(2)}) %copy-start.4) | copy-done | bytes 2097176
  59.0 0.4 fusion.10
  59.8 1.1 %fusion.81 = f32[128,512]{0,1:T(8,128)} fusion(bf16[2,2,512,512]{3,2,1,0:T(8,128)(2,1)S(1)} %copy-done, bf16[2,512,128]{2,1,0:T(8,128)(2,1)S(1)} %bitcast.365), kind=kOutput, calls=%fused_computation.140 | convolution fusion | flops 67108864 | bytes 917504 | tf_op jit(solution)/shard_map/...nm,...nk->...mk/dot_general | solution.py:95
  61.3 1.4 %fusion.71 = (f32[2,1,512,128]{3,2,1,0:T(8,128)}, f32[2,1,512,128]{3,2,1,0:T(8,128)}, bf16[2,128,512]{1,2,0:T(8,128)(2,1)S(1)}) fusion(f32[2,512]{1,0:T(2,128)S(1)} %get-tuple-element.33, f32[2,512]{1,0:T(2,128)S(1)} %get-tuple-element.34, bf16[2,128,512]{1,2,0:T(8,128)(2,1)S(1)} %fusion.10, f32[2,128,512]{1,2,0:T(8,128)S(1)} %fusion.141, ...), kind=kOutput, calls=%fused_computation.117 | convolution fusion | flops 135528448 | bytes 3416064 | tf_op jit(solution)/shard_map/...mn,...nk->...mk/dot_general | solution.py:91
  62.7 1.0 %fusion.79 = f32[128,512]{0,1:T(8,128)} fusion(bf16[2,2,512,512]{3,2,1,0:T(8,128)(2,1)S(1)} %copy-done, bf16[2,512,128]{2,1,0:T(8,128)(2,1)S(1)} %bitcast.374), kind=kOutput, calls=%fused_computation.138 | convolution fusion | flops 67108864 | bytes 917504 | tf_op jit(solution)/shard_map/...nm,...nk->...mk/dot_general | solution.py:95
  64.8 0.7 pad_maximum_fusion.10.hand_ref
  65.6 0.9 fusion.123
  66.4 12.5 %exchange_2.1 = (bf16[2,512,128]{2,1,0:T(8,128)(2,1)}, bf16[2,512,128]{2,1,0:T(8,128)(2,1)}) custom-call(bf16[2,512,128]{2,1,0:T(8,128)(2,1)} %get-tuple-element.23.st0_ref, bf16[2,512,128]{2,1,0:T(8,128)(2,1)} %pad_maximum_fusion.10.hand_ref), custom_call_target="tpu_custom_call" | custom-call | tf_op jit(solution)/shard_map/exchange_2/pallas_call | solution.py:74
  79.0 1.5 %fusion.63 = f32[2,128,512]{1,2,0:T(8,128)S(1)} fusion(bf16[2,2,512,512]{3,2,1,0:T(8,128)(2,1)S(1)} %copy-done, bf16[1,2,512,128]{3,2,1,0:T(8,128)(2,1)} %get-tuple-element.22, bf16[1,2,512,128]{3,2,1,0:T(8,128)(2,1)} %bitcast.393), kind=kOutput, calls=%fused_computation.96 | convolution fusion | flops 134742016 | bytes 2097152 | tf_op jit(solution)/shard_map/...mn,...nk->...mk/dot_general | solution.py:91
  80.5 0.4 fusion.65
  81.8 0.4 fusion.1
  82.3 0.4 fusion
  83.3 1.4 %copy-done.5 = bf16[1,2,2,512,512]{4,3,1,2,0:T(8,128)(2,1)S(1)} copy-done((bf16[1,2,2,512,512]{4,3,1,2,0:T(8,128)(2,1)S(1)}, bf16[1,2,2,512,512]{4,3,1,2,0:T(8,128)(2,1)}, u32[]{:S(2)}) %copy-start.5) | copy-done | bytes 2097176
  85.1 0.4 fusion.143
  85.5 0.4 fusion.15
  86.0 0.5 fusion.14
  86.5 3.7 %collective-permute-start = (bf16[2,512,256]{2,1,0:T(8,128)(2,1)S(1)}, bf16[2,512,256]{2,1,0:T(8,128)(2,1)S(1)}, u32[]{:S(2)}, u32[]{:S(2)}) collective-permute-start(bf16[2,512,256]{2,1,0:T(8,128)(2,1)S(1)} %get-tuple-element.21), channel_id=1, source_target_pairs={{0,128},{128,0},{1,129},{129,1},{2,130},{130,2},{3,131},{131,3},{4... | collective-permute-start | bytes 1572872 | tf_op jit(solution)/shard_map/ppermute | solution.py:128
  90.2 1.5 %collective-permute-done = bf16[2,512,256]{2,1,0:T(8,128)(2,1)S(1)} collective-permute-done((bf16[2,512,256]{2,1,0:T(8,128)(2,1)S(1)}, bf16[2,512,256]{2,1,0:T(8,128)(2,1)S(1)}, u32[]{:S(2)}, u32[]{:S(2)}) %collective-permute-start) | collective-permute-done | bytes 524320 | tf_op jit(solution)/shard_map/ppermute | solution.py:128
  91.8 1.1 %pad_maximum_fusion.both_ref = bf16[2,2,512,256]{3,2,1,0:T(8,128)(2,1)} fusion(bf16[1,2,512,256]{3,2,1,0:T(8,128)(2,1)S(1)} %bitcast.397, bf16[1,2,512,256]{3,2,1,0:T(8,128)(2,1)S(1)} %get-tuple-element.20), kind=kLoop, calls=%fused_computation.81 | loop fusion | flops 524288 | bytes 2097152 | tf_op jit(solution)/shard_map/stack | solution.py:129
  92.9 4.7 %shard_map.86 = (bf16[1,2,2,512,512]{4,3,2,1,0:T(8,128)(2,1)}, bf16[1,2,2,512,512]{4,3,2,1,0:T(8,128)(2,1)}) custom-call(bf16[2,2,512,256]{3,2,1,0:T(8,128)(2,1)} %pad_maximum_fusion.both_ref, f32[2,128]{1,0:T(2,128)} %occ_ref.1, s32[2,4]{1,0:T(2,128)} %off_ref.1, f32[2,4]{1,0:T(2,128)} %wt_ref.1), custom_call_target="tpu_custom_call" | custom-call | tf_op jit(solution)/shard_map/pallas_call | solution.py:173
  (83 shorter events, 10.7 us)
Async XLA Ops:
  3.7 3.1 %copy-start.2 = (bf16[1,2,2,512,512]{4,3,1,2,0:T(8,128)(2,1)}, bf16[1,2,2,512,512]{4,3,1,2,0:T(8,128)(2,1)S(1)}, u32[]{:S(2)}) copy-start(bf16[1,2,2,512,512]{4,3,1,2,0:T(8,128)(2,1)S(1)} %copy.238) | copy-start | bytes 6291460
  4.1 1.9 %copy-start = (bf16[2,2,512,512]{3,2,1,0:T(8,128)(2,1)S(1)}, bf16[2,2,512,512]{3,2,1,0:T(8,128)(2,1)}, u32[]{:S(2)}) copy-start(bf16[2,2,512,512]{3,2,1,0:T(8,128)(2,1)} %param.8) | copy-start | bytes 6291460
  4.6 2.1 %copy-start.28 = (f32[1,2,2,512]{3,2,1,0:T(2,128)S(1)}, f32[1,2,2,512]{3,2,1,0:T(2,128)}, u32[]{:S(2)}) copy-start(f32[1,2,2,512]{3,2,1,0:T(2,128)} %param.10) | copy-start | bytes 24580
  25.5 1.4 %copy-start.18 = (bf16[2,512,128]{2,1,0:T(8,128)(2,1)S(1)}, bf16[2,512,128]{2,1,0:T(8,128)(2,1)}, u32[]{:S(2)}) copy-start(bf16[2,512,128]{2,1,0:T(8,128)(2,1)} %get-tuple-element.8) | copy-start | bytes 786436
  28.1 1.2 %copy-start.1 = (f32[1,2,2,512,128]{4,3,2,1,0:T(8,128)S(1)}, f32[1,2,2,512,128]{4,3,2,1,0:T(8,128)}, u32[]{:S(2)}) copy-start(f32[1,2,2,512,128]{4,3,2,1,0:T(8,128)} %param.9) | copy-start | bytes 3145732
  28.1 1.3 %copy-start.14 = (f32[2,1,512,128]{3,2,1,0:T(8,128)S(1)}, f32[2,1,512,128]{3,2,1,0:T(8,128)}, u32[]{:S(2)}) copy-start(f32[2,1,512,128]{3,2,1,0:T(8,128)} %get-tuple-element.18) | copy-start | bytes 1572868
  28.1 1.5 %copy-start.15 = (f32[2,1,512,128]{3,2,1,0:T(8,128)S(1)}, f32[2,1,512,128]{3,2,1,0:T(8,128)}, u32[]{:S(2)}) copy-start(f32[2,1,512,128]{3,2,1,0:T(8,128)} %get-tuple-element.19) | copy-start | bytes 1572868
  28.1 1.5 %copy-start.25 = (bf16[2,512,128]{2,1,0:T(8,128)(2,1)S(1)}, bf16[2,512,128]{2,1,0:T(8,128)(2,1)}, u32[]{:S(2)}) copy-start(bf16[2,512,128]{2,1,0:T(8,128)(2,1)} %get-tuple-element.9) | copy-start | bytes 786436
  29.7 1.6 %copy-start.3 = (bf16[1,2,2,512,512]{4,3,1,2,0:T(8,128)(2,1)S(1)}, bf16[1,2,2,512,512]{4,3,1,2,0:T(8,128)(2,1)}, u32[]{:S(2)}) copy-start(bf16[1,2,2,512,512]{4,3,1,2,0:T(8,128)(2,1)} %copy-done.2) | copy-start | bytes 6291460
  35.4 2.9 %copy-start.8 = (bf16[2,128,512]{1,2,0:T(8,128)(2,1)}, bf16[2,128,512]{1,2,0:T(8,128)(2,1)S(1)}, u32[]{:S(2)}) copy-start(bf16[2,128,512]{1,2,0:T(8,128)(2,1)S(1)} %get-tuple-element.31) | copy-start | bytes 786436
  52.9 1.5 %copy-start.10 = (bf16[1,2,512,128]{3,2,1,0:T(8,128)(2,1)S(1)}, bf16[1,2,512,128]{3,2,1,0:T(8,128)(2,1)}, u32[]{:S(2)}) copy-start(bf16[1,2,512,128]{3,2,1,0:T(8,128)(2,1)} %get-tuple-element.24) | copy-start | bytes 786436
  52.9 1.5 %copy-start.19 = (bf16[2,512,128]{2,1,0:T(8,128)(2,1)S(1)}, bf16[2,512,128]{2,1,0:T(8,128)(2,1)}, u32[]{:S(2)}) copy-start(bf16[2,512,128]{2,1,0:T(8,128)(2,1)} %get-tuple-element.10) | copy-start | bytes 786436
  52.9 2.0 %copy-start.9 = (bf16[2,128,512]{1,2,0:T(8,128)(2,1)S(1)}, bf16[2,128,512]{1,2,0:T(8,128)(2,1)}, u32[]{:S(2)}) copy-start(bf16[2,128,512]{1,2,0:T(8,128)(2,1)} %copy-done.8) | copy-start | bytes 786436
  52.9 2.0 %copy-start.22 = (f32[128,512]{0,1:T(8,128)S(1)}, f32[128,512]{0,1:T(8,128)}, u32[]{:S(2)}) copy-start(f32[128,512]{0,1:T(8,128)} %fusion.85) | copy-start | bytes 786436
  54.4 1.0 copy-start.23
  55.7 1.0 %copy-start.16 = (f32[2,1,512,128]{3,2,1,0:T(8,128)S(1)}, f32[2,1,512,128]{3,2,1,0:T(8,128)}, u32[]{:S(2)}) copy-start(f32[2,1,512,128]{3,2,1,0:T(8,128)} %get-tuple-element.16) | copy-start | bytes 1572868
  55.7 1.2 %copy-start.17 = (f32[2,1,512,128]{3,2,1,0:T(8,128)S(1)}, f32[2,1,512,128]{3,2,1,0:T(8,128)}, u32[]{:S(2)}) copy-start(f32[2,1,512,128]{3,2,1,0:T(8,128)} %get-tuple-element.17) | copy-start | bytes 1572868
  55.7 1.2 %copy-start.26 = (bf16[2,512,128]{2,1,0:T(8,128)(2,1)S(1)}, bf16[2,512,128]{2,1,0:T(8,128)(2,1)}, u32[]{:S(2)}) copy-start(bf16[2,512,128]{2,1,0:T(8,128)(2,1)} %get-tuple-element.11) | copy-start | bytes 786436
  57.0 1.6 %copy-start.4 = (bf16[1,2,2,512,512]{4,3,1,2,0:T(8,128)(2,1)S(1)}, bf16[1,2,2,512,512]{4,3,1,2,0:T(8,128)(2,1)}, u32[]{:S(2)}) copy-start(bf16[1,2,2,512,512]{4,3,1,2,0:T(8,128)(2,1)} %copy-done.2) | copy-start | bytes 6291460
  62.7 2.8 %copy-start.6 = (bf16[2,128,512]{1,2,0:T(8,128)(2,1)}, bf16[2,128,512]{1,2,0:T(8,128)(2,1)S(1)}, u32[]{:S(2)}) copy-start(bf16[2,128,512]{1,2,0:T(8,128)(2,1)S(1)} %get-tuple-element.32) | copy-start | bytes 786436
  79.0 1.5 %copy-start.11 = (bf16[1,2,512,128]{3,2,1,0:T(8,128)(2,1)S(1)}, bf16[1,2,512,128]{3,2,1,0:T(8,128)(2,1)}, u32[]{:S(2)}) copy-start(bf16[1,2,512,128]{3,2,1,0:T(8,128)(2,1)} %get-tuple-element.22) | copy-start | bytes 786436
  79.0 1.5 %copy-start.20 = (bf16[2,512,128]{2,1,0:T(8,128)(2,1)S(1)}, bf16[2,512,128]{2,1,0:T(8,128)(2,1)}, u32[]{:S(2)}) copy-start(bf16[2,512,128]{2,1,0:T(8,128)(2,1)} %get-tuple-element.12) | copy-start | bytes 786436
  79.0 2.0 %copy-start.7 = (bf16[2,128,512]{1,2,0:T(8,128)(2,1)S(1)}, bf16[2,128,512]{1,2,0:T(8,128)(2,1)}, u32[]{:S(2)}) copy-start(bf16[2,128,512]{1,2,0:T(8,128)(2,1)} %copy-done.6) | copy-start | bytes 786436
  79.0 2.0 %copy-start.21 = (f32[128,512]{0,1:T(8,128)S(1)}, f32[128,512]{0,1:T(8,128)}, u32[]{:S(2)}) copy-start(f32[128,512]{0,1:T(8,128)} %fusion.81) | copy-start | bytes 786436
  80.5 1.0 copy-start.24
  81.8 1.0 %copy-start.12 = (f32[2,1,512,128]{3,2,1,0:T(8,128)S(1)}, f32[2,1,512,128]{3,2,1,0:T(8,128)}, u32[]{:S(2)}) copy-start(f32[2,1,512,128]{3,2,1,0:T(8,128)} %get-tuple-element.14) | copy-start | bytes 1572868
  81.8 1.2 %copy-start.13 = (f32[2,1,512,128]{3,2,1,0:T(8,128)S(1)}, f32[2,1,512,128]{3,2,1,0:T(8,128)}, u32[]{:S(2)}) copy-start(f32[2,1,512,128]{3,2,1,0:T(8,128)} %get-tuple-element.15) | copy-start | bytes 1572868
  81.8 1.2 %copy-start.27 = (bf16[2,512,128]{2,1,0:T(8,128)(2,1)S(1)}, bf16[2,512,128]{2,1,0:T(8,128)(2,1)}, u32[]{:S(2)}) copy-start(bf16[2,512,128]{2,1,0:T(8,128)(2,1)} %get-tuple-element.13) | copy-start | bytes 786436
  83.1 1.6 %copy-start.5 = (bf16[1,2,2,512,512]{4,3,1,2,0:T(8,128)(2,1)S(1)}, bf16[1,2,2,512,512]{4,3,1,2,0:T(8,128)(2,1)}, u32[]{:S(2)}) copy-start(bf16[1,2,2,512,512]{4,3,1,2,0:T(8,128)(2,1)} %copy-done.2) | copy-start | bytes 6291460
  86.5 5.2 %collective-permute-start = (bf16[2,512,256]{2,1,0:T(8,128)(2,1)S(1)}, bf16[2,512,256]{2,1,0:T(8,128)(2,1)S(1)}, u32[]{:S(2)}, u32[]{:S(2)}) collective-permute-start(bf16[2,512,256]{2,1,0:T(8,128)(2,1)S(1)} %get-tuple-element.21), channel_id=1, source_target_pairs={{0,128},{128,0},{1,129},{129,1},{2,130},{130,2},{3,131},{131,3},{4... | collective-permute-start | bytes 1572872 | tf_op jit(solution)/shard_map/ppermute | solution.py:128

commit v6 on v4

--- a/solution.py
+++ b/solution.py
@@ -17,15 +17,19 @@
     return jnp.dot(a, b, preferred_element_type=F32)
 
 
+def nt_dot(a, b):
+    return lax.dot_general(a, b, (((1,), (1,)), ((), ())), preferred_element_type=F32)
+
+
 def solve_kernel(n, chunks, pre_hbm, cpl_hbm, src_hbm, sig_ref, out_ref,
-                 pre, cpl, src, srcc, ct, st, follow, arrive, hand, other, part,
+                 pre, cpl, src, srcc, st, follow, arrive, hand, other, part,
                  load_sem, send_sem, recv_sem, swap_sem):
     me = lax.axis_index("space")
     en = lax.axis_index("energy")
     prev = lax.rem(me + n - 1, n)
     nxt = lax.rem(me + 1, n)
     mate = 1 - en
-    w = st.shape[-1]
+    w = st.shape[-2]
     h = w // 2
 
     loads = [pltpu.make_async_copy(src_hbm.at[0], src, load_sem.at[0])]
@@ -47,29 +51,22 @@
     def _():
         arrive[...] = jnp.zeros_like(arrive)
 
-    lanes = lax.broadcasted_iota(jnp.int32, (1, w), 1)
-    low = lanes < h
-    neg_low = jnp.where(low, -1.0, 1.0).astype(F32)
-
-    def turn(x):
-        return pltpu.roll(x, h, 1)
-
-    def column(s):
-        g = jnp.concatenate([sig_ref[0, s], jnp.zeros((6, sig_ref.shape[-1]), F32)], axis=0).T
-        return g[:, 0:1], g[:, 1:2]
-
-    sig = [column(s) for s in range(2)]
-
     def cprod(mr, mi, rhs):
-        return dot(mr, rhs) + neg_low * turn(dot(mi, rhs))
+        x = nt_dot(rhs, mr)
+        y = nt_dot(rhs, mi)
+        return jnp.concatenate([x[:h] - y[h:], x[h:] + y[:h]], axis=0)
 
     def cprod_adj(mr, mi, rhs):
-        return dot(mr, rhs) - neg_low * turn(dot(mi, rhs))
+        x = dot(rhs, mr)
+        y = dot(rhs, mi)
+        return jnp.concatenate([x[:h] + y[h:], x[h:] - y[:h]], axis=0)
 
     def local(c, s):
         x = st[c, s].astype(F32)
-        gr, gi = sig[s]
-        return srcc[c, s] + (gr * x + (gi * neg_low) * turn(x))
+        xr, xi = x[:h], x[h:]
+        gr = sig_ref[0, s, pl.ds(0, 1), :]
+        gi = sig_ref[0, s, pl.ds(1, 1), :]
+        return srcc[c, s] + jnp.concatenate([gr * xr - gi * xi, gr * xi + gi * xr], axis=0)
 
     sweeps = SWEEPS - 1
 
@@ -88,10 +85,10 @@
 
     loads[0].wait()
     for s in range(2):
-        re = src[s, 0]
-        im = src[s, 1]
-        srcc[0, s] = jnp.where(low, re, turn(im))
-        srcc[1, s] = jnp.where(low, turn(re), im)
+        re = src[s, 0].T
+        im = src[s, 1].T
+        for c in range(chunks):
+            srcc[c, s] = jnp.concatenate([re[c * h:(c + 1) * h], im[c * h:(c + 1) * h]], axis=0)
 
     for s in range(2):
         loads[1 + s].wait()
@@ -104,18 +101,16 @@
 
     for s in range(2):
         loads[3 + s].wait()
-        for p in range(2):
-            ct[s, p] = cpl[s, p].T
 
     def phase1(sweep, c):
         to_prev, to_next = copies[sweep][c]
-        hand[sweep, c] = cprod_adj(ct[1, 0], ct[1, 1], st[c, 1]).astype(BF16)
+        hand[sweep, c] = cprod_adj(cpl[1, 0], cpl[1, 1], st[c, 1]).astype(BF16)
 
         @pl.when(me < n - 1)
         def _():
             to_next.start()
 
-        part[c, 2] = cprod_adj(ct[0, 0], ct[0, 1], st[c, 0]).astype(BF16).astype(F32)
+        part[c, 2] = cprod_adj(cpl[0, 0], cpl[0, 1], st[c, 0]).astype(BF16).astype(F32)
         part[c, 1] = local(c, 1)
         part[c, 0] = local(c, 0) + cprod(cpl[0, 0], cpl[0, 1], st[c, 1])
 
@@ -167,18 +162,18 @@
 
     for c in range(chunks):
         for s in range(2):
-            out_ref[0, s, :, c * w:(c + 1) * w] = st[c, s]
+            out_ref[0, s, :, c * w:(c + 1) * w] = st[c, s].T
     for c in range(chunks):
         swaps[c].wait()
         for s in range(2):
-            out_ref[1, s, :, c * w:(c + 1) * w] = other[c, s]
+            out_ref[1, s, :, c * w:(c + 1) * w] = other[c, s].T
 
 
 def solve(precond, coupling, source, sigma, n):
     m, h = source.shape[-2:]
     chunks = 2
     sweeps = SWEEPS - 1
-    blk = (m, 2 * h // chunks)
+    blk = (2 * h // chunks, m)
     vmem = pl.BlockSpec(memory_space=pltpu.VMEM)
     anyspace = pl.BlockSpec(memory_space=pl.ANY)
     return pl.pallas_call(
@@ -191,7 +186,6 @@
             pltpu.VMEM(coupling.shape, BF16),
             pltpu.VMEM(source.shape[1:], F32),
             pltpu.VMEM((chunks, 2) + blk, F32),
-            pltpu.VMEM(coupling.shape, BF16),
             pltpu.VMEM((chunks, 2) + blk, BF16),
             pltpu.VMEM((sweeps, chunks) + blk, BF16),
             pltpu.VMEM((sweeps, chunks) + blk, BF16),
@@ -205,10 +199,6 @@
         ],
         compiler_params=pltpu.CompilerParams(collective_id=0, has_side_effects=True),
     )(precond, coupling, source, sigma)
-
-
-def nt_dot(a, b):
-    return lax.dot_general(a, b, (((1,), (1,)), ((), ())), preferred_element_type=F32)
 
 
 def self_kernel(both_ref, occ_ref, off_ref, wt_ref, less_ref, great_ref):

time: 45.4 us -> 44 us (0.969)
  Pallas kernels: 44.7 us -> 43.2 us
    pallas_call x1, Pallas kernels: 39.8 us -> 38.3 us  [solve(): pl.pallas_call(functools.partial(solve_kernel, n, chunks), out_shape=jax....]
where the time goes in v6:
time: 44 us; the launch traced here: 43.8 us
  Pallas kernels  43.2 us (98%)
  between operations  0.64 us (1%)
    pallas_call x1, Pallas kernels, solve(): pl.pallas_call(functools.partial(solve_kernel, n, chunks), out_shape=jax....  38.3 us
    pallas_call x1, Pallas kernels, self_energy(): pl.pallas_call(self_kernel, out_shape=(shape, shape), grid=(2,), in_specs...  4.88 us

profile of v6, /device:TPU:129, one launch (start us, length us, event | category | flops | bytes accessed | tf_op | source)
XLA Modules:
  0.0 43.8 jit_solution(1205417330568580107)
XLA Ops:
  0.6 38.3 %shard_map.86.both_ref = bf16[2,2,512,256]{3,2,1,0:T(8,128)(2,1)} custom-call(bf16[1,2,2,512,512]{4,3,2,1,0:T(8,128)(2,1)} %pre_hbm.1, bf16[2,2,512,512]{3,2,1,0:T(8,128)(2,1)} %cpl_hbm.1, f32[1,2,2,512,128]{4,3,2,1,0:T(8,128)} %src_hbm.1, f32[1,2,2,512]{3,2,1,0:T(2,128)} %sig_ref.1), custom_call_target="tpu_custom_call" | custom-call | tf_op jit(solution)/shard_map/pallas_call | solution.py:179
  39.0 4.9 %shard_map.87 = (bf16[1,2,2,512,512]{4,3,2,1,0:T(8,128)(2,1)}, bf16[1,2,2,512,512]{4,3,2,1,0:T(8,128)(2,1)}) custom-call(bf16[2,2,512,256]{3,2,1,0:T(8,128)(2,1)} %shard_map.86.both_ref, f32[2,128]{1,0:T(2,128)} %occ_ref.1, s32[2,4]{1,0:T(2,128)} %off_ref.1, f32[2,4]{1,0:T(2,128)} %wt_ref.1), custom_call_target="tpu_custom_call" | custom-call | tf_op jit(solution)/shard_map/pallas_call | solution.py:250

commit v7 on v6

--- a/solution.py
+++ b/solution.py
@@ -21,7 +21,8 @@
     return lax.dot_general(a, b, (((1,), (1,)), ((), ())), preferred_element_type=F32)
 
 
-def solve_kernel(n, chunks, pre_hbm, cpl_hbm, src_hbm, sig_ref, out_ref,
+def solve_kernel(n, chunks, pre_hbm, cpl_hbm, src_hbm, sig_ref, occ_ref, off_ref, wt_ref,
+                 out_ref, scale_ref,
                  pre, cpl, src, srcc, st, follow, arrive, hand, other, part,
                  load_sem, send_sem, recv_sem, swap_sem):
     me = lax.axis_index("space")
@@ -42,6 +43,8 @@
     for peer in ((en, prev), (en, nxt), (mate, me)):
         pl.semaphore_signal(barrier, inc=1, device_id=peer, device_id_type=MESH)
     pl.semaphore_wait(barrier, 3)
+
+    shift_scales(occ_ref, off_ref, wt_ref, scale_ref)
 
     @pl.when(me == n - 1)
     def _():
@@ -169,18 +172,20 @@
             out_ref[1, s, :, c * w:(c + 1) * w] = other[c, s].T
 
 
-def solve(precond, coupling, source, sigma, n):
+def solve(precond, coupling, source, sigma, occupation, shift_offsets, shift_weights, n):
     m, h = source.shape[-2:]
     chunks = 2
     sweeps = SWEEPS - 1
     blk = (2 * h // chunks, m)
     vmem = pl.BlockSpec(memory_space=pltpu.VMEM)
     anyspace = pl.BlockSpec(memory_space=pl.ANY)
+    smem = pl.BlockSpec(memory_space=pltpu.SMEM)
     return pl.pallas_call(
         functools.partial(solve_kernel, n, chunks),
-        out_shape=jax.ShapeDtypeStruct((2, 2, m, 2 * h), BF16),
-        in_specs=[anyspace, anyspace, anyspace, vmem],
-        out_specs=vmem,
+        out_shape=(jax.ShapeDtypeStruct((2, 2, m, 2 * h), BF16),
+                   jax.ShapeDtypeStruct((2, 1, 4 * h), F32)),
+        in_specs=[anyspace, anyspace, anyspace, vmem, vmem, smem, smem],
+        out_specs=(vmem, vmem),
         scratch_shapes=[
             pltpu.VMEM(precond.shape[1:], BF16),
             pltpu.VMEM(coupling.shape, BF16),
@@ -198,11 +203,11 @@
             pltpu.SemaphoreType.DMA((2, chunks)),
         ],
         compiler_params=pltpu.CompilerParams(collective_id=0, has_side_effects=True),
-    )(precond, coupling, source, sigma)
-
-
-def self_kernel(both_ref, occ_ref, off_ref, wt_ref, less_ref, great_ref):
-    h = both_ref.shape[-1] // 2
+    )(precond, coupling, source, sigma, occupation, shift_offsets, shift_weights)
+
+
+def shift_scales(occ_ref, off_ref, wt_ref, scale_ref):
+    h = occ_ref.shape[-1]
     energy_total = occ_ref.shape[0]
     e = lax.axis_index("energy")
     mate = 1 - e
@@ -218,7 +223,6 @@
     occ_mate = occ_ref[pl.ds(mate, 1), :]
     lanes = lax.broadcasted_iota(jnp.int32, (1, h), 1)
     low = lanes < h // 2
-    pos_low = jnp.where(low, 1.0, -1.0).astype(BF16)
 
     def turn(x):
         return pltpu.roll(x, h // 2, 1)
@@ -226,45 +230,33 @@
     def spread(v):
         return jnp.concatenate([jnp.where(low, v, turn(v)), jnp.where(low, turn(v), v)], axis=1)
 
-    scales = []
-    for own_part, mate_part in ((occ_own, occ_mate), (1.0 - occ_own, 1.0 - occ_mate)):
-        scales.append(jnp.concatenate([spread(coef_own * own_part), spread(coef_mate * mate_part)], axis=1))
-    own = both_ref[0, 0]
-    mate_states = both_ref[1, 0]
-    a = jnp.concatenate([own, mate_states], axis=1)
-    blocks = [x[:, i * h:(i + 1) * h] for x in (own, mate_states) for i in range(2)]
-    swapped = jnp.concatenate(
-        [(turn(b.astype(F32)) * pos_low.astype(F32)).astype(BF16) for b in blocks], axis=1)
+    pairs = ((occ_own, occ_mate), (1.0 - occ_own, 1.0 - occ_mate))
+    for q, (own_part, mate_part) in enumerate(pairs):
+        scale_ref[q] = jnp.concatenate(
+            [spread(coef_own * own_part), spread(coef_mate * mate_part)], axis=1)
+
+
+def self_energy(both, scales):
+    a = jnp.concatenate([both[0], both[1]], axis=-1)
+    s, m, k = a.shape
+    width = both.shape[-1] // 2
+    halves = a.reshape(s, m, k // width, 2, width // 2)
+    swapped = jnp.stack([halves[:, :, :, 1], -halves[:, :, :, 0]], axis=3).reshape(s, m, k)
+    lhs = jnp.stack([a, swapped], axis=1)
     af = a.astype(F32)
-    for scale, out in zip(scales, (less_ref, great_ref)):
-        b = (af * scale).astype(BF16)
-        out[0, 0, 0] = nt_dot(a, b).astype(BF16)
-        out[0, 0, 1] = nt_dot(swapped, b).astype(BF16)
-
-
-def self_energy(both, occupation, shift_offsets, shift_weights):
-    m, w = both.shape[2:]
-    shape = jax.ShapeDtypeStruct((1, 2, 2, m, m), BF16)
-    smem = pl.BlockSpec(memory_space=pltpu.SMEM)
-    out_spec = pl.BlockSpec((1, 1, 2, m, m), lambda s: (0, s, 0, 0, 0))
-    return pl.pallas_call(
-        self_kernel,
-        out_shape=(shape, shape),
-        grid=(2,),
-        in_specs=[
-            pl.BlockSpec((2, 1, m, w), lambda s: (0, s, 0, 0)),
-            pl.BlockSpec(occupation.shape, lambda s: (0, 0)),
-            smem,
-            smem,
-        ],
-        out_specs=(out_spec, out_spec),
-    )(both, occupation, shift_offsets, shift_weights)
+    outs = []
+    for i in range(2):
+        b = (af * scales[i]).astype(BF16)
+        out = jnp.einsum("scmk,snk->scmn", lhs, b, preferred_element_type=F32)
+        outs.append(out.astype(BF16)[None])
+    return tuple(outs)
 
 
 def body(precond, coupling, source, sigma_ret, occupation, shift_offsets, shift_weights):
     n = lax.axis_size("space")
-    both = solve(precond, coupling, source, sigma_ret, n)
-    return self_energy(both, occupation, shift_offsets, shift_weights)
+    both, scales = solve(precond, coupling, source, sigma_ret, occupation, shift_offsets,
+                         shift_weights, n)
+    return self_energy(both, scales)
 
 
 def solution(mesh):

time: 44 us -> 47.9 us (1.089)
  matrix products: 0 us -> 5.22 us
  Pallas kernels: 43.2 us -> 38.5 us
  local copies, waits for them, and re-layouts: 0 us -> 2.98 us
    dot_general x0 -> x2, matrix products: none -> 5.22 us  [self_energy(): out = jnp.einsum('scmk,snk->scmn', lhs, b, preferred_element_type=F32)]
    pallas_call x2 -> x1, Pallas kernels: 43.2 us -> 38.5 us  [solve(): pl.pallas_call(functools.partial(solve_kernel, n, chunks), out_shape=(jax...]
    squeeze x0 -> x1, local copies, waits for them, and re-layouts: none -> 1.33 us  [self_energy(): a = jnp.concatenate([both[0], both[1]], axis=-1)]
    slice x0 -> x3, local copies, waits for them, and re-layouts: none -> 1.1 us  [the longest x1 0.68 us: self_energy(): b = (af * scales[i]).astype(BF16)]
    another operation x0 -> x1, local copies, waits for them, and re-layouts: none -> 0.54 us  [self_energy(): lhs = jnp.stack([a, swapped], axis=1)]
where the time goes in v7:
time: 47.9 us; the launch traced here: 47.7 us
  Pallas kernels  38.5 us (80%)
  matrix products  5.22 us (11%)
  local copies, waits for them, and re-layouts  2.98 us (6%)
  between operations  0.69 us (1%)
    pallas_call x1, Pallas kernels, solve(): pl.pallas_call(functools.partial(solve_kernel, n, chunks), out_shape=(jax...  38.5 us
    dot_general x2, matrix products, self_energy(): out = jnp.einsum('scmk,snk->scmn', lhs, b, preferred_element_type=F32)  5.22 us
    squeeze x1, local copies, waits for them, and re-layouts, self_energy(): a = jnp.concatenate([both[0], both[1]], axis=-1)  1.33 us

profile of v7, /device:TPU:129, one launch (start us, length us, event | category | flops | bytes accessed | tf_op | source)
XLA Modules:
  0.0 47.7 jit_solution(14938265728175993197)
XLA Ops:
  0.6 38.5 %shard_map.86 = (bf16[2,2,512,256]{3,2,1,0:T(8,128)(2,1)}, f32[2,1,512]{2,1,0:T(1,128)}) custom-call(bf16[1,2,2,512,512]{4,3,2,1,0:T(8,128)(2,1)} %pre_hbm.1, bf16[2,2,512,512]{3,2,1,0:T(8,128)(2,1)} %cpl_hbm.1, f32[1,2,2,512,128]{4,3,2,1,0:T(8,128)} %src_hbm.1, f32[1,2,2,512]{3,2,1,0:T(2,128)} %sig_ref.1, f32[2,128]{1,0:T(2,128)} %occ_ref.1, ...), custom_call_target="tpu_custom_call" | custom-call | tf_op jit(solution)/shard_map/pallas_call | solution.py:183
  39.2 0.7 %fusion.15 = (f32[1,1,512]{2,1,0:T(1,128)S(1)}, f32[1,1,512]{2,1,0:T(1,128)S(1)}) fusion(f32[2,1,512]{2,1,0:T(1,128)} %get-tuple-element.5), kind=kLoop, calls=%fused_computation.25 | loop fusion | bytes 8192 | tf_op jit(solution)/shard_map/slice | solution.py:249
  39.9 1.3 %slice_bitcast_fusion.1 = (bf16[2,512,256]{2,1,0:T(8,128)(2,1)S(1)}, bf16[2,512,256]{2,1,0:T(8,128)(2,1)S(1)}, bf16[1,2,512,256]{3,2,1,0:T(8,128)(2,1)S(1)}, bf16[1,2,512,256]{3,2,1,0:T(8,128)(2,1)S(1)}) fusion(bf16[2,2,512,256]{3,2,1,0:T(8,128)(2,1)} %get-tuple-element.4), kind=kLoop, calls=%fused_computation.24 | loop fusion | bytes 3145728 | tf_op jit(solution)/shard_map/squeeze | solution.py:240
  41.2 0.2 copy.12
  41.4 0.2 copy.11
  41.6 0.1 fusion.10
  41.8 0.1 pad_maximum_fusion.2
  41.9 0.5 %copy.13 = bf16[2,1,512,512]{3,2,0,1:T(8,128)(2,1)S(1)} copy(bf16[2,1,512,512]{2,3,0,1:T(8,128)(2,1)S(1)} %bitcast.25) | data formatting | bytes 2097152 | tf_op jit(solution)/shard_map/stack;reshape | solution.py:245
  42.4 0.1 fusion.12
  42.5 2.6 %convert_bitcast_fusion = bf16[1,2,2,512,512]{4,3,2,1,0:T(8,128)(2,1)} fusion(f32[512]{0:T(512)S(1)} %bitcast.29, bf16[2,512,256]{2,1,0:T(8,128)(2,1)S(1)} %get-tuple-element.7, bf16[2,512,256]{2,1,0:T(8,128)(2,1)S(1)} %get-tuple-element.6, bf16[2,1,512,512]{3,2,0,1:T(8,128)(2,1)S(1)} %copy.13, bf16[2,1,512,512]{3,2,0,1:T(8,128)(2,1)S(1)} %fusion.12), kind=kOutput, calls=%fused_computation.5 | convolution fusion | flops 1078984704 | bytes 5244928 | tf_op jit(solution)/shard_map/scmk,snk->scmn/dot_general | solution.py:250
  45.1 2.6 %convert_bitcast_fusion.1 = bf16[1,2,2,512,512]{4,3,2,1,0:T(8,128)(2,1)} fusion(f32[512]{0:T(512)S(1)} %bitcast.28, bf16[2,512,256]{2,1,0:T(8,128)(2,1)S(1)} %get-tuple-element.7, bf16[2,512,256]{2,1,0:T(8,128)(2,1)S(1)} %get-tuple-element.6, bf16[2,1,512,512]{3,2,0,1:T(8,128)(2,1)S(1)} %copy.13, bf16[2,1,512,512]{3,2,0,1:T(8,128)(2,1)S(1)} %fusion.12), kind=kOutput, calls=%fused_computation.6 | convolution fusion | flops 1078984704 | bytes 5244928 | tf_op jit(solution)/shard_map/scmk,snk->scmn/dot_general | solution.py:250

commit v8 on v6

--- a/solution.py
+++ b/solution.py
@@ -160,18 +160,27 @@
             else:
                 swaps[c].start()
 
+    q = out_ref.shape[-1] // 4
+    per = h // q
+
+    def put(i, ref, c):
+        for s in range(2):
+            x = ref[c, s]
+            for b in range(per):
+                rows = jnp.concatenate([x[b * q:(b + 1) * q], x[h + b * q:h + (b + 1) * q]], axis=0)
+                lo = (c * per + b) * 2 * q
+                out_ref[i, s, :, lo:lo + 2 * q] = rows.T
+
     for c in range(chunks):
-        for s in range(2):
-            out_ref[0, s, :, c * w:(c + 1) * w] = st[c, s].T
+        put(0, st, c)
     for c in range(chunks):
         swaps[c].wait()
-        for s in range(2):
-            out_ref[1, s, :, c * w:(c + 1) * w] = other[c, s].T
+        put(1, other, c)
 
 
 def solve(precond, coupling, source, sigma, n):
     m, h = source.shape[-2:]
-    chunks = 2
+    chunks = 1
     sweeps = SWEEPS - 1
     blk = (2 * h // chunks, m)
     vmem = pl.BlockSpec(memory_space=pltpu.VMEM)

time: 44 us -> 46.1 us (1.048)
  Pallas kernels: 43.2 us -> 45.3 us
    pallas_call x1, Pallas kernels: 38.3 us -> 40.4 us  [solve(): pl.pallas_call(functools.partial(solve_kernel, n, chunks), out_shape=jax....]
where the time goes in v8:
time: 46.1 us; the launch traced here: 45.9 us
  Pallas kernels  45.3 us (98%)
  between operations  0.64 us (1%)
    pallas_call x1, Pallas kernels, solve(): pl.pallas_call(functools.partial(solve_kernel, n, chunks), out_shape=jax....  40.4 us
    pallas_call x1, Pallas kernels, self_energy(): pl.pallas_call(self_kernel, out_shape=(shape, shape), grid=(2,), in_specs...  4.88 us

profile of v8, /device:TPU:129, one launch (start us, length us, event | category | flops | bytes accessed | tf_op | source)
XLA Modules:
  0.0 45.9 jit_solution(2453626491635551131)
XLA Ops:
  0.6 40.4 %shard_map.86.both_ref = bf16[2,2,512,256]{3,2,1,0:T(8,128)(2,1)} custom-call(bf16[1,2,2,512,512]{4,3,2,1,0:T(8,128)(2,1)} %pre_hbm.1, bf16[2,2,512,512]{3,2,1,0:T(8,128)(2,1)} %cpl_hbm.1, f32[1,2,2,512,128]{4,3,2,1,0:T(8,128)} %src_hbm.1, f32[1,2,2,512]{3,2,1,0:T(2,128)} %sig_ref.1), custom_call_target="tpu_custom_call" | custom-call | tf_op jit(solution)/shard_map/pallas_call | solution.py:188
  41.0 4.9 %shard_map.87 = (bf16[1,2,2,512,512]{4,3,2,1,0:T(8,128)(2,1)}, bf16[1,2,2,512,512]{4,3,2,1,0:T(8,128)(2,1)}) custom-call(bf16[2,2,512,256]{3,2,1,0:T(8,128)(2,1)} %shard_map.86.both_ref, f32[2,128]{1,0:T(2,128)} %occ_ref.1, s32[2,4]{1,0:T(2,128)} %off_ref.1, f32[2,4]{1,0:T(2,128)} %wt_ref.1), custom_call_target="tpu_custom_call" | custom-call | tf_op jit(solution)/shard_map/pallas_call | solution.py:259

commit v9 on v6

--- a/solution.py
+++ b/solution.py
@@ -236,10 +236,13 @@
     swapped = jnp.concatenate(
         [(turn(b.astype(F32)) * pos_low.astype(F32)).astype(BF16) for b in blocks], axis=1)
     af = a.astype(F32)
+    lhs = jnp.concatenate([a, swapped], axis=0)
+    m = a.shape[0]
     for scale, out in zip(scales, (less_ref, great_ref)):
         b = (af * scale).astype(BF16)
-        out[0, 0, 0] = nt_dot(a, b).astype(BF16)
-        out[0, 0, 1] = nt_dot(swapped, b).astype(BF16)
+        both = nt_dot(lhs, b)
+        out[0, 0, 0] = both[:m].astype(BF16)
+        out[0, 0, 1] = both[m:].astype(BF16)
 
 
 def self_energy(both, occupation, shift_offsets, shift_weights):

time: 44 us -> 44 us (level)
  no operation moved by 1% of the time
where the time goes in v9:
time: 44 us; the launch traced here: 43.9 us
  Pallas kernels  43.2 us (98%)
  between operations  0.64 us (1%)
    pallas_call x1, Pallas kernels, solve(): pl.pallas_call(functools.partial(solve_kernel, n, chunks), out_shape=jax....  38.3 us
    pallas_call x1, Pallas kernels, self_energy(): pl.pallas_call(self_kernel, out_shape=(shape, shape), grid=(2,), in_specs...  4.89 us

profile of v9, /device:TPU:129, one launch (start us, length us, event | category | flops | bytes accessed | tf_op | source)
XLA Modules:
  0.0 43.9 jit_solution(388136103074244100)
XLA Ops:
  0.6 38.3 %shard_map.86.both_ref = bf16[2,2,512,256]{3,2,1,0:T(8,128)(2,1)} custom-call(bf16[1,2,2,512,512]{4,3,2,1,0:T(8,128)(2,1)} %pre_hbm.1, bf16[2,2,512,512]{3,2,1,0:T(8,128)(2,1)} %cpl_hbm.1, f32[1,2,2,512,128]{4,3,2,1,0:T(8,128)} %src_hbm.1, f32[1,2,2,512]{3,2,1,0:T(2,128)} %sig_ref.1), custom_call_target="tpu_custom_call" | custom-call | tf_op jit(solution)/shard_map/pallas_call | solution.py:179
  39.0 4.9 %shard_map.87 = (bf16[1,2,2,512,512]{4,3,2,1,0:T(8,128)(2,1)}, bf16[1,2,2,512,512]{4,3,2,1,0:T(8,128)(2,1)}) custom-call(bf16[2,2,512,256]{3,2,1,0:T(8,128)(2,1)} %shard_map.86.both_ref, f32[2,128]{1,0:T(2,128)} %occ_ref.1, s32[2,4]{1,0:T(2,128)} %off_ref.1, f32[2,4]{1,0:T(2,128)} %wt_ref.1), custom_call_target="tpu_custom_call" | custom-call | tf_op jit(solution)/shard_map/pallas_call | solution.py:253

commit v10 on v9

--- a/solution.py
+++ b/solution.py
@@ -92,8 +92,13 @@
 
     for s in range(2):
         loads[1 + s].wait()
+        rhs = jnp.concatenate([srcc[c, s] for c in range(chunks)], axis=0).astype(BF16)
+        x = nt_dot(rhs, pre[s, 0])
+        y = nt_dot(rhs, pre[s, 1])
         for c in range(chunks):
-            st[c, s] = cprod(pre[s, 0], pre[s, 1], srcc[c, s].astype(BF16)).astype(BF16)
+            lo, mid, hi = c * w, c * w + h, (c + 1) * w
+            st[c, s] = jnp.concatenate(
+                [x[lo:mid] - y[mid:hi], x[mid:hi] + y[lo:mid]], axis=0).astype(BF16)
             if s == 0:
                 @pl.when(me > 0)
                 def _():

time: 44 us -> 43.2 us (0.982)
  Pallas kernels: 43.2 us -> 42.4 us
    pallas_call x1, Pallas kernels: 38.3 us -> 37.5 us  [solve(): pl.pallas_call(functools.partial(solve_kernel, n, chunks), out_shape=jax....]
where the time goes in v10:
time: 43.2 us; the launch traced here: 43 us
  Pallas kernels  42.4 us (98%)
  between operations  0.64 us (1%)
    pallas_call x1, Pallas kernels, solve(): pl.pallas_call(functools.partial(solve_kernel, n, chunks), out_shape=jax....  37.5 us
    pallas_call x1, Pallas kernels, self_energy(): pl.pallas_call(self_kernel, out_shape=(shape, shape), grid=(2,), in_specs...  4.89 us

profile of v10, /device:TPU:129, one launch (start us, length us, event | category | flops | bytes accessed | tf_op | source)
XLA Modules:
  0.0 43.0 jit_solution(7310529858716678876)
XLA Ops:
  0.6 37.5 %shard_map.86.both_ref = bf16[2,2,512,256]{3,2,1,0:T(8,128)(2,1)} custom-call(bf16[1,2,2,512,512]{4,3,2,1,0:T(8,128)(2,1)} %pre_hbm.1, bf16[2,2,512,512]{3,2,1,0:T(8,128)(2,1)} %cpl_hbm.1, f32[1,2,2,512,128]{4,3,2,1,0:T(8,128)} %src_hbm.1, f32[1,2,2,512]{3,2,1,0:T(2,128)} %sig_ref.1), custom_call_target="tpu_custom_call" | custom-call | tf_op jit(solution)/shard_map/pallas_call | solution.py:184
  38.1 4.9 %shard_map.87 = (bf16[1,2,2,512,512]{4,3,2,1,0:T(8,128)(2,1)}, bf16[1,2,2,512,512]{4,3,2,1,0:T(8,128)(2,1)}) custom-call(bf16[2,2,512,256]{3,2,1,0:T(8,128)(2,1)} %shard_map.86.both_ref, f32[2,128]{1,0:T(2,128)} %occ_ref.1, s32[2,4]{1,0:T(2,128)} %off_ref.1, f32[2,4]{1,0:T(2,128)} %wt_ref.1), custom_call_target="tpu_custom_call" | custom-call | tf_op jit(solution)/shard_map/pallas_call | solution.py:258

commit v11 on v10

--- a/solution.py
+++ b/solution.py
@@ -155,8 +155,29 @@
         recv_sem=swap_sem.at[1, c], device_id=(mate, me), device_id_type=MESH)
         for c in range(chunks)]
 
+    def both_rows(c, x, y, sign):
+        lo, mid, hi = c * w, c * w + h, (c + 1) * w
+        return jnp.concatenate([x[lo:mid] - sign * y[mid:hi], x[mid:hi] + sign * y[lo:mid]], axis=0)
+
+    rows1 = jnp.concatenate([st[c, 1] for c in range(chunks)], axis=0)
+    rows0 = jnp.concatenate([st[c, 0] for c in range(chunks)], axis=0)
+    hx = dot(rows1, cpl[1, 0])
+    hy = dot(rows1, cpl[1, 1])
     for c in range(chunks):
-        phase1(0, c)
+        hand[0, c] = both_rows(c, hx, hy, -1.0).astype(BF16)
+
+        @pl.when(me < n - 1)
+        def _():
+            copies[0][c][1].start()
+
+    lx = dot(rows0, cpl[0, 0])
+    ly = dot(rows0, cpl[0, 1])
+    ux = nt_dot(rows1, cpl[0, 0])
+    uy = nt_dot(rows1, cpl[0, 1])
+    for c in range(chunks):
+        part[c, 2] = both_rows(c, lx, ly, -1.0).astype(BF16).astype(F32)
+        part[c, 1] = local(c, 1)
+        part[c, 0] = local(c, 0) + both_rows(c, ux, uy, 1.0)
     for sweep in range(sweeps):
         for c in range(chunks):
             phase2(sweep, c)

time: 43.2 us -> 43.3 us (level)
  no operation moved by 1% of the time
where the time goes in v11:
time: 43.3 us; the launch traced here: 43.2 us
  Pallas kernels  42.5 us (98%)
  between operations  0.64 us (1%)
    pallas_call x1, Pallas kernels, solve(): pl.pallas_call(functools.partial(solve_kernel, n, chunks), out_shape=jax....  37.6 us
    pallas_call x1, Pallas kernels, self_energy(): pl.pallas_call(self_kernel, out_shape=(shape, shape), grid=(2,), in_specs...  4.89 us

profile of v11, /device:TPU:129, one launch (start us, length us, event | category | flops | bytes accessed | tf_op | source)
XLA Modules:
  0.0 43.2 jit_solution(8382314213105909723)
XLA Ops:
  0.6 37.6 %shard_map.86.both_ref = bf16[2,2,512,256]{3,2,1,0:T(8,128)(2,1)} custom-call(bf16[1,2,2,512,512]{4,3,2,1,0:T(8,128)(2,1)} %pre_hbm.1, bf16[2,2,512,512]{3,2,1,0:T(8,128)(2,1)} %cpl_hbm.1, f32[1,2,2,512,128]{4,3,2,1,0:T(8,128)} %src_hbm.1, f32[1,2,2,512]{3,2,1,0:T(2,128)} %sig_ref.1), custom_call_target="tpu_custom_call" | custom-call | tf_op jit(solution)/shard_map/pallas_call | solution.py:205
  38.3 4.9 %shard_map.87 = (bf16[1,2,2,512,512]{4,3,2,1,0:T(8,128)(2,1)}, bf16[1,2,2,512,512]{4,3,2,1,0:T(8,128)(2,1)}) custom-call(bf16[2,2,512,256]{3,2,1,0:T(8,128)(2,1)} %shard_map.86.both_ref, f32[2,128]{1,0:T(2,128)} %occ_ref.1, s32[2,4]{1,0:T(2,128)} %off_ref.1, f32[2,4]{1,0:T(2,128)} %wt_ref.1), custom_call_target="tpu_custom_call" | custom-call | tf_op jit(solution)/shard_map/pallas_call | solution.py:279

commit v12 on v10

--- a/solution.py
+++ b/solution.py
@@ -164,10 +164,9 @@
                 phase1(sweep + 1, c)
             else:
                 swaps[c].start()
-
-    for c in range(chunks):
-        for s in range(2):
-            out_ref[0, s, :, c * w:(c + 1) * w] = st[c, s].T
+                for s in range(2):
+                    out_ref[0, s, :, c * w:(c + 1) * w] = st[c, s].T
+
     for c in range(chunks):
         swaps[c].wait()
         for s in range(2):

time: 43.2 us -> 43.2 us (level)
  no operation moved by 1% of the time
where the time goes in v12:
time: 43.2 us; the launch traced here: 43 us
  Pallas kernels  42.4 us (98%)
  between operations  0.64 us (1%)
    pallas_call x1, Pallas kernels, solve(): pl.pallas_call(functools.partial(solve_kernel, n, chunks), out_shape=jax....  37.5 us
    pallas_call x1, Pallas kernels, self_energy(): pl.pallas_call(self_kernel, out_shape=(shape, shape), grid=(2,), in_specs...  4.89 us

profile of v12, /device:TPU:129, one launch (start us, length us, event | category | flops | bytes accessed | tf_op | source)
XLA Modules:
  0.0 43.0 jit_solution(4248285491330760209)
XLA Ops:
  0.6 37.5 %shard_map.86.both_ref = bf16[2,2,512,256]{3,2,1,0:T(8,128)(2,1)} custom-call(bf16[1,2,2,512,512]{4,3,2,1,0:T(8,128)(2,1)} %pre_hbm.1, bf16[2,2,512,512]{3,2,1,0:T(8,128)(2,1)} %cpl_hbm.1, f32[1,2,2,512,128]{4,3,2,1,0:T(8,128)} %src_hbm.1, f32[1,2,2,512]{3,2,1,0:T(2,128)} %sig_ref.1), custom_call_target="tpu_custom_call" | custom-call | tf_op jit(solution)/shard_map/pallas_call | solution.py:183
  38.1 4.9 %shard_map.87 = (bf16[1,2,2,512,512]{4,3,2,1,0:T(8,128)(2,1)}, bf16[1,2,2,512,512]{4,3,2,1,0:T(8,128)(2,1)}) custom-call(bf16[2,2,512,256]{3,2,1,0:T(8,128)(2,1)} %shard_map.86.both_ref, f32[2,128]{1,0:T(2,128)} %occ_ref.1, s32[2,4]{1,0:T(2,128)} %off_ref.1, f32[2,4]{1,0:T(2,128)} %wt_ref.1), custom_call_target="tpu_custom_call" | custom-call | tf_op jit(solution)/shard_map/pallas_call | solution.py:257

commit v13 on v12

--- a/solution.py
+++ b/solution.py
@@ -41,7 +41,6 @@
     barrier = pltpu.get_barrier_semaphore()
     for peer in ((en, prev), (en, nxt), (mate, me)):
         pl.semaphore_signal(barrier, inc=1, device_id=peer, device_id_type=MESH)
-    pl.semaphore_wait(barrier, 3)
 
     @pl.when(me == n - 1)
     def _():
@@ -99,7 +98,9 @@
             lo, mid, hi = c * w, c * w + h, (c + 1) * w
             st[c, s] = jnp.concatenate(
                 [x[lo:mid] - y[mid:hi], x[mid:hi] + y[lo:mid]], axis=0).astype(BF16)
-            if s == 0:
+        if s == 0:
+            pl.semaphore_wait(barrier, 3)
+            for c in range(chunks):
                 @pl.when(me > 0)
                 def _():
                     copies[0][c][0].start()

time: 43.2 us -> 42.3 us (0.979)
  Pallas kernels: 42.4 us -> 41.6 us
    pallas_call x1, Pallas kernels: 37.5 us -> 36.7 us  [solve(): pl.pallas_call(functools.partial(solve_kernel, n, chunks), out_shape=jax....]
where the time goes in v13:
time: 42.3 us; the launch traced here: 42.2 us
  Pallas kernels  41.6 us (98%)
  between operations  0.64 us (2%)
    pallas_call x1, Pallas kernels, solve(): pl.pallas_call(functools.partial(solve_kernel, n, chunks), out_shape=jax....  36.7 us
    pallas_call x1, Pallas kernels, self_energy(): pl.pallas_call(self_kernel, out_shape=(shape, shape), grid=(2,), in_specs...  4.89 us

profile of v13, /device:TPU:129, one launch (start us, length us, event | category | flops | bytes accessed | tf_op | source)
XLA Modules:
  0.0 42.2 jit_solution(88056336941137024)
XLA Ops:
  0.6 36.7 %shard_map.86.both_ref = bf16[2,2,512,256]{3,2,1,0:T(8,128)(2,1)} custom-call(bf16[1,2,2,512,512]{4,3,2,1,0:T(8,128)(2,1)} %pre_hbm.1, bf16[2,2,512,512]{3,2,1,0:T(8,128)(2,1)} %cpl_hbm.1, f32[1,2,2,512,128]{4,3,2,1,0:T(8,128)} %src_hbm.1, f32[1,2,2,512]{3,2,1,0:T(2,128)} %sig_ref.1), custom_call_target="tpu_custom_call" | custom-call | tf_op jit(solution)/shard_map/pallas_call | solution.py:184
  37.3 4.9 %shard_map.87 = (bf16[1,2,2,512,512]{4,3,2,1,0:T(8,128)(2,1)}, bf16[1,2,2,512,512]{4,3,2,1,0:T(8,128)(2,1)}) custom-call(bf16[2,2,512,256]{3,2,1,0:T(8,128)(2,1)} %shard_map.86.both_ref, f32[2,128]{1,0:T(2,128)} %occ_ref.1, s32[2,4]{1,0:T(2,128)} %off_ref.1, f32[2,4]{1,0:T(2,128)} %wt_ref.1), custom_call_target="tpu_custom_call" | custom-call | tf_op jit(solution)/shard_map/pallas_call | solution.py:258

commit v14 on v12

--- a/solution.py
+++ b/solution.py
@@ -41,7 +41,6 @@
     barrier = pltpu.get_barrier_semaphore()
     for peer in ((en, prev), (en, nxt), (mate, me)):
         pl.semaphore_signal(barrier, inc=1, device_id=peer, device_id_type=MESH)
-    pl.semaphore_wait(barrier, 3)
 
     @pl.when(me == n - 1)
     def _():
@@ -99,10 +98,12 @@
             lo, mid, hi = c * w, c * w + h, (c + 1) * w
             st[c, s] = jnp.concatenate(
                 [x[lo:mid] - y[mid:hi], x[mid:hi] + y[lo:mid]], axis=0).astype(BF16)
-            if s == 0:
-                @pl.when(me > 0)
-                def _():
-                    copies[0][c][0].start()
+
+    pl.semaphore_wait(barrier, 3)
+    for c in range(chunks):
+        @pl.when(me > 0)
+        def _():
+            copies[0][c][0].start()
 
     for s in range(2):
         loads[3 + s].wait()

time: 43.2 us -> 42 us (0.972)
  Pallas kernels: 42.4 us -> 41.2 us
    pallas_call x1, Pallas kernels: 37.5 us -> 36.4 us  [solve(): pl.pallas_call(functools.partial(solve_kernel, n, chunks), out_shape=jax....]
where the time goes in v14:
time: 42 us; the launch traced here: 41.9 us
  Pallas kernels  41.2 us (98%)
  between operations  0.64 us (2%)
    pallas_call x1, Pallas kernels, solve(): pl.pallas_call(functools.partial(solve_kernel, n, chunks), out_shape=jax....  36.4 us
    pallas_call x1, Pallas kernels, self_energy(): pl.pallas_call(self_kernel, out_shape=(shape, shape), grid=(2,), in_specs...  4.89 us

profile of v14, /device:TPU:129, one launch (start us, length us, event | category | flops | bytes accessed | tf_op | source)
XLA Modules:
  0.0 41.9 jit_solution(4135415313174121281)
XLA Ops:
  0.6 36.4 %shard_map.86.both_ref = bf16[2,2,512,256]{3,2,1,0:T(8,128)(2,1)} custom-call(bf16[1,2,2,512,512]{4,3,2,1,0:T(8,128)(2,1)} %pre_hbm.1, bf16[2,2,512,512]{3,2,1,0:T(8,128)(2,1)} %cpl_hbm.1, f32[1,2,2,512,128]{4,3,2,1,0:T(8,128)} %src_hbm.1, f32[1,2,2,512]{3,2,1,0:T(2,128)} %sig_ref.1), custom_call_target="tpu_custom_call" | custom-call | tf_op jit(solution)/shard_map/pallas_call | solution.py:184
  37.0 4.9 %shard_map.87 = (bf16[1,2,2,512,512]{4,3,2,1,0:T(8,128)(2,1)}, bf16[1,2,2,512,512]{4,3,2,1,0:T(8,128)(2,1)}) custom-call(bf16[2,2,512,256]{3,2,1,0:T(8,128)(2,1)} %shard_map.86.both_ref, f32[2,128]{1,0:T(2,128)} %occ_ref.1, s32[2,4]{1,0:T(2,128)} %off_ref.1, f32[2,4]{1,0:T(2,128)} %wt_ref.1), custom_call_target="tpu_custom_call" | custom-call | tf_op jit(solution)/shard_map/pallas_call | solution.py:258
